TPU v7x, 32 devices: a whole 2x2x4 slice. The times are simulated.
32 devices in a mesh: blk: 4 (over z), uly: 8 (over y, x, core).
Axes of the slice: x: 2, y: 2, z: 4, core: 2. Of those that a mesh axis runs over, the one named last changes fastest.
Arguments:
- queries: bfloat16 [4096, 4096], P(('blk', 'uly')), may hold values from -6 to 6
- keys: bfloat16 [4096, 1024], P(('blk', 'uly')), may hold values from -6 to 6
- values: bfloat16 [4096, 1024], P(('blk', 'uly')), may hold values from -6 to 6
- grad_out: bfloat16 [4096, 4096], P(('blk', 'uly')), may hold values from -6 to 6
- row_delta: float32 [4096, 32], P(('blk', 'uly')), may hold values from -18 to 18
- doc_ids: int32 [4096], replicated, may hold values from 0 to 63, never falling along the last dimension, each value on 1 to 128 neighbouring positions
- doc_lang: int32 [64], replicated, may hold values from 0 to 3
- tile_list: int32 [8, 32, 2], replicated, may hold values from 0 to 31, as said below
Outputs:
- grad_queries: bfloat16 [4096, 4096], P(('blk', 'uly'))
- grad_keys: bfloat16 [4096, 1024], P(('blk', 'uly'))
- grad_values: bfloat16 [4096, 1024], P(('blk', 'uly'))
Inputs may be any that keep to these rules, and one draw needn't show every extreme that they name: `doc_ids`: document ids never fall, rise by one where a new document begins, and a document holds at most 128 tokens. `tile_list`: each listed tile of query tile a is at most a and not before the first tile of the block of 8 tiles that precedes the block of a; entries may repeat.
All inputs are finite; a program needn't handle non-finite values.
Results may differ from a plain program's by a relative error of at most 0.0059.
Values may be sent and summed in bfloat16 or wider, within the bound.
A program may use at most 128 MiB of HBM per device.

v0:
```python
import math

import jax
import jax.numpy as jnp
from jax import lax
from jax.sharding import PartitionSpec as P

DH = 128
BLOCK = 128


MASKED = -1e30


def from_behind(block, axis, distance):
    devices = range(lax.axis_size(axis))
    route = [(i - distance, i) for i in devices if i - distance in devices]
    return lax.ppermute(block, axis, route)


def candidates(list_group, query_tiles):
    band_tiles = query_tiles[:, None] + jnp.arange(-1, 1, dtype=jnp.int32)[None, :]
    listed = jnp.take(list_group, query_tiles, axis=0, mode="clip")
    list_count = listed.shape[1]
    in_band = jnp.any(listed[:, :, None] == band_tiles[:, None, :], axis=2)
    earlier = jnp.tril(jnp.ones((list_count, list_count), jnp.bool_), -1)
    repeated = jnp.any((listed[:, :, None] == listed[:, None, :]) & earlier[None], axis=2)
    candidate = jnp.concatenate([band_tiles, listed], axis=1)
    usable = jnp.concatenate([band_tiles >= 0, jnp.logical_not(in_band | repeated)], axis=1)
    marked = jnp.any(candidate[:, :, None] == listed[:, None, :], axis=2)
    return (candidate, usable, marked)


def allowed_tiles(candidate, usable, marked, query_tiles, doc_ids, position_lang):
    offsets = jnp.arange(BLOCK, dtype=jnp.int32)
    query_pos = query_tiles[:, None] * BLOCK + offsets[None, :]
    key_pos = jnp.maximum(candidate, 0)[:, :, None] * BLOCK + offsets[None, None, :]
    query_doc = jnp.take(doc_ids, query_pos, mode="clip")
    key_doc = jnp.take(doc_ids, key_pos, mode="clip")
    query_lang = jnp.take(position_lang, query_pos, mode="clip")
    key_lang = jnp.take(position_lang, key_pos, mode="clip")
    causal = key_pos[:, :, None, :] <= query_pos[:, None, :, None]
    same_doc = key_doc[:, :, None, :] == query_doc[:, None, :, None]
    same_lang = key_lang[:, :, None, :] == query_lang[:, None, :, None]
    return usable[:, :, None, None] & causal & (same_doc | same_lang & marked[:, :, None, None])


def tile_setup(
    list_group, first_query, window_first, slot_count, tile_group, doc_ids, position_lang
):
    query_tiles = first_query + jnp.arange(tile_group, dtype=jnp.int32)
    candidate, usable, marked = candidates(list_group, query_tiles)
    window_slot = candidate - window_first
    usable = usable & (window_slot >= 0) & (window_slot < slot_count)
    window_slot = jnp.clip(window_slot, 0, slot_count - 1)
    allowed = allowed_tiles(candidate, usable, marked, query_tiles, doc_ids, position_lang)
    return (window_slot, allowed)


def tile_stats(query_part, key_part, allowed, scaling):
    scores = scaling * jnp.einsum(
        "qid,qcjd->qcij", query_part, key_part, preferred_element_type=jnp.float32
    )
    masked = jnp.where(allowed, scores, MASKED)
    row_top = jnp.max(masked, axis=(1, 3))
    row_total = jnp.sum(
        jnp.where(allowed, jnp.exp(masked - row_top[:, None, :, None]), 0.0), axis=(1, 3)
    )
    return row_top + jnp.log(row_total)


def tile_grads(
    query_part, dout_part, key_part, value_part, log_total, delta_part, allowed, scaling
):
    scores = scaling * jnp.einsum(
        "qid,qcjd->qcij", query_part, key_part, preferred_element_type=jnp.float32
    )
    weights = jnp.where(allowed, jnp.exp(scores - log_total[:, None, :, None]), 0.0)
    weights_low = weights.astype(jnp.bfloat16)
    grad_value = jnp.einsum(
        "qcij,qid->qcjd", weights_low, dout_part, preferred_element_type=jnp.float32
    )
    grad_weights = jnp.einsum(
        "qid,qcjd->qcij", dout_part, value_part, preferred_element_type=jnp.float32
    )
    grad_scores = (weights * (grad_weights - delta_part[:, None, :, None])).astype(jnp.bfloat16)
    grad_query = scaling * jnp.einsum(
        "qcij,qcjd->qid", grad_scores, key_part, preferred_element_type=jnp.float32
    )
    grad_key = scaling * jnp.einsum(
        "qcij,qid->qcjd", grad_scores, query_part, preferred_element_type=jnp.float32
    )
    return (grad_query, grad_key, grad_value)


def stats_pass(
    query_one,
    key_tiles,
    list_group,
    first_tile,
    window_first,
    doc_ids,
    position_lang,
    tile_group,
    scaling,
):
    slot_count = key_tiles.shape[0]
    tile_count = query_one.shape[0] // BLOCK

    def stats_step(tile_start):
        window_slot, allowed = tile_setup(
            list_group,
            first_tile + tile_start,
            window_first,
            slot_count,
            tile_group,
            doc_ids,
            position_lang,
        )
        query_part = lax.dynamic_slice_in_dim(
            query_one, tile_start * BLOCK, tile_group * BLOCK
        ).reshape(tile_group, BLOCK, DH)
        key_part = jnp.take(key_tiles, window_slot, axis=0)
        return tile_stats(query_part, key_part, allowed, scaling)

    tile_starts = jnp.arange(tile_count // tile_group, dtype=jnp.int32) * tile_group
    return lax.map(stats_step, tile_starts).reshape(tile_count * BLOCK)


def grad_pass(
    query_one,
    dout_one,
    lse_one,
    delta_one,
    key_tiles,
    value_tiles,
    list_group,
    first_tile,
    window_first,
    doc_ids,
    position_lang,
    tile_group,
    scaling,
):
    slot_count = key_tiles.shape[0]
    tile_count = query_one.shape[0] // BLOCK

    def scan_step(carried, tile_start):
        key_sum, value_sum = carried
        window_slot, allowed = tile_setup(
            list_group,
            first_tile + tile_start,
            window_first,
            slot_count,
            tile_group,
            doc_ids,
            position_lang,
        )
        row_start = tile_start * BLOCK
        row_span = tile_group * BLOCK
        query_part = lax.dynamic_slice_in_dim(query_one, row_start, row_span).reshape(
            tile_group, BLOCK, DH
        )
        dout_part = lax.dynamic_slice_in_dim(dout_one, row_start, row_span).reshape(
            tile_group, BLOCK, DH
        )
        lse_part = lax.dynamic_slice_in_dim(lse_one, row_start, row_span).reshape(tile_group, BLOCK)
        delta_part = lax.dynamic_slice_in_dim(delta_one, row_start, row_span).reshape(
            tile_group, BLOCK
        )
        key_part = jnp.take(key_tiles, window_slot, axis=0)
        value_part = jnp.take(value_tiles, window_slot, axis=0)
        grad_query, grad_key, grad_value = tile_grads(
            query_part, dout_part, key_part, value_part, lse_part, delta_part, allowed, scaling
        )
        flat_slot = window_slot.reshape(-1)
        key_sum = key_sum.at[flat_slot].add(grad_key.reshape(-1, BLOCK, DH))
        value_sum = value_sum.at[flat_slot].add(grad_value.reshape(-1, BLOCK, DH))
        return ((key_sum, value_sum), grad_query)

    zero_tiles = jnp.zeros((slot_count, BLOCK, DH), jnp.float32)
    tile_starts = jnp.arange(tile_count // tile_group, dtype=jnp.int32) * tile_group
    sums, grad_query = lax.scan(scan_step, (zero_tiles, zero_tiles), tile_starts)
    return (grad_query.reshape(-1, DH), sums[0].reshape(-1, DH), sums[1].reshape(-1, DH))


def widened(packed, groups_all, repeat_count):
    tok_count = packed.shape[0]
    spread = jnp.broadcast_to(
        packed.reshape(tok_count, groups_all, 1, DH), (tok_count, groups_all, repeat_count, DH)
    )
    return spread.reshape(tok_count, groups_all * repeat_count * DH)


def shards(queries, keys, values, grad_out, row_delta, doc_ids, doc_lang, tile_list):
    tok_count, full_width = queries.shape
    heads_all = full_width // DH
    groups_all = keys.shape[1] // DH
    repeat_count = heads_all // groups_all
    group_size = lax.axis_size("uly")
    heads_here = heads_all // group_size
    row_count = tok_count * group_size
    tiles_here = row_count // BLOCK
    tile_group = math.gcd(tiles_here, 4)
    scaling = float(DH) ** (-0.5)
    query_heads, dout_heads, key_heads, value_heads = (
        lax.all_to_all(queries, "uly", split_axis=1, concat_axis=0, tiled=True),
        lax.all_to_all(grad_out, "uly", split_axis=1, concat_axis=0, tiled=True),
        lax.all_to_all(
            widened(keys, groups_all, repeat_count), "uly", split_axis=1, concat_axis=0, tiled=True
        ),
        lax.all_to_all(
            widened(values, groups_all, repeat_count),
            "uly",
            split_axis=1,
            concat_axis=0,
            tiled=True,
        ),
    )
    delta_heads = lax.all_to_all(row_delta, "uly", split_axis=1, concat_axis=0, tiled=True)
    earlier_key, earlier_value = from_behind((key_heads, value_heads), "blk", 1)
    key_window = jnp.concatenate([earlier_key, key_heads], axis=0)
    value_window = jnp.concatenate([earlier_value, value_heads], axis=0)
    block_index = lax.axis_index("blk")
    head_base = lax.axis_index("uly") * heads_here
    position_lang = jnp.take(doc_lang, doc_ids, mode="clip")
    first_tile = block_index * tiles_here
    window_first = (block_index - 1) * tiles_here

    def column(array, head):
        return array[:, head * DH : (head + 1) * DH]

    lse_list = []
    query_list = []
    key_list = []
    value_list = []
    for head in range(heads_here):
        list_group = jnp.take(tile_list, (head_base + head) // repeat_count, axis=0)
        key_tiles = column(key_window, head).reshape(2 * tiles_here, BLOCK, DH)
        value_tiles = column(value_window, head).reshape(2 * tiles_here, BLOCK, DH)
        query_one = column(query_heads, head)
        log_total = stats_pass(
            query_one,
            key_tiles,
            list_group,
            first_tile,
            window_first,
            doc_ids,
            position_lang,
            tile_group,
            scaling,
        )
        grad_query, key_sum, value_sum = grad_pass(
            query_one,
            column(dout_heads, head),
            log_total,
            delta_heads[:, head],
            key_tiles,
            value_tiles,
            list_group,
            first_tile,
            window_first,
            doc_ids,
            position_lang,
            tile_group,
            scaling,
        )
        lse_list.append(log_total)
        query_list.append(grad_query)
        key_list.append(key_sum)
        value_list.append(value_sum)
    grad_query_all = jnp.concatenate(query_list, axis=1)
    key_window_sum = jnp.concatenate(key_list, axis=1)
    value_window_sum = jnp.concatenate(value_list, axis=1)
    returned_key, returned_value = from_behind(
        (key_window_sum[:row_count], value_window_sum[:row_count]), "blk", -1
    )
    key_total = key_window_sum[row_count:] + returned_key
    value_total = value_window_sum[row_count:] + returned_value
    grad_queries, key_tokens, value_tokens = (
        lax.all_to_all(
            grad_query_all.astype(jnp.bfloat16), "uly", split_axis=0, concat_axis=1, tiled=True
        ),
        lax.all_to_all(
            key_total.astype(jnp.bfloat16), "uly", split_axis=0, concat_axis=1, tiled=True
        ),
        lax.all_to_all(
            value_total.astype(jnp.bfloat16), "uly", split_axis=0, concat_axis=1, tiled=True
        ),
    )

    def folded(per_head):
        summed = jnp.sum(
            per_head.astype(jnp.float32).reshape(tok_count, groups_all, repeat_count, DH), axis=2
        )
        return summed.reshape(tok_count, groups_all * DH).astype(jnp.bfloat16)

    return (grad_queries, folded(key_tokens), folded(value_tokens))


def solution(mesh):
    placed = (
        P(("blk", "uly"), None),
        P(("blk", "uly"), None),
        P(("blk", "uly"), None),
        P(("blk", "uly"), None),
        P(("blk", "uly"), None),
        P(),
        P(),
        P(),
    )
    return jax.shard_map(
        shards,
        mesh=mesh,
        in_specs=placed,
        out_specs=(P(("blk", "uly"), None), P(("blk", "uly"), None), P(("blk", "uly"), None)),
        check_vma=False,
    )
```

profile of v0, /device:TPU:0, one launch (start us, length us, event | category | flops | bytes accessed | tf_op | source)
XLA Modules:
  0.0 955.2 jit_solution(10773038753303476912)
XLA Ops:
  0.6 5.3 all-to-all-start.4
  10.7 3.6 all-to-all-start
  15.4 14.2 %all-to-all-done = bf16[128,8,512]{2,0,1:T(8,128)(2,1)S(1)} async-done(((bf16[128,8,512]{2,0,1:T(8,128)(2,1)}), bf16[128,8,512]{2,0,1:T(8,128)(2,1)S(1)}, u32[]{:S(2)}, u32[]{:S(2)}) %all-to-all-start) | async-done | bytes 1048608 | tf_op jit(solution)/shard_map/all_to_all | solution.py:209
  29.6 3.6 all-to-all-start.1
  34.8 13.7 %all-to-all-done.1 = bf16[128,8,512]{2,0,1:T(8,128)(2,1)S(1)} async-done(((bf16[128,8,512]{2,0,1:T(8,128)(2,1)}), bf16[128,8,512]{2,0,1:T(8,128)(2,1)S(1)}, u32[]{:S(2)}, u32[]{:S(2)}) %all-to-all-start.1) | async-done | bytes 1048608 | tf_op jit(solution)/shard_map/all_to_all | solution.py:207
  48.5 3.6 all-to-all-start.2
  57.0 10.4 %all-to-all-done.2 = bf16[128,8,512]{2,0,1:T(8,128)(2,1)S(1)} async-done(((bf16[128,8,512]{2,0,1:T(8,128)(2,1)}), bf16[128,8,512]{2,0,1:T(8,128)(2,1)S(1)}, u32[]{:S(2)}, u32[]{:S(2)}) %all-to-all-start.2) | async-done | bytes 1048608 | tf_op jit(solution)/shard_map/all_to_all | solution.py:212
  67.4 3.6 all-to-all-start.3
  71.7 4.5 collective-permute-start
  76.2 39.9 %select_select_fusion = s32[4096]{0:T(1024)S(1)} fusion(s32[4096]{0:T(1024)S(1)} %copy-done.2, s32[]{:T(128)} %bitcast.169, s32[]{:T(128)} %bitcast.170, s32[]{:T(128)} %bitcast.171, s32[]{:T(128)} %bitcast.172, s32[]{:T(128)} %bitcast.173, s32[]{:T(128)} %bitcast.174, s32[]{:T(128)} %bitcast.175, s32[]{:T(128)} %bitcast.176, s32[]{:T(128)} %bitcast.177, ...), kind=kLoop, calls=%fused_computation.463 | loop fusion | flops 516096 | bytes 33024 | tf_op jit(solution)/shard_map/jit(_take)/gather | solution.py:226
  116.7 4.0 collective-permute-start.1
  125.8 75.9 %while.97 = (s32[]{:T(128)}, f32[2,4,128]{2,1,0:T(4,128)S(1)}, s32[2]{0:T(128)S(1)}, s32[]{:T(128)}, s32[32,2]{1,0:T(8,128)S(1)}, /*index=5*/s32[]{:T(128)}, s32...) while((s32[]{:T(128)}, f32[2,4,128]{2,1,0:T(4,128)S(1)}, ...), condition=%wide.region_6.9_spmd, body=%wide.region_0.8_spmd.sunk | while | flops 72624064 | bytes 4251355 | solution.py:127
  129.5 11.8 %gather_fusion.3 = s32[2048]{0:T(1024)S(1)} fusion(s32[4096]{0:T(1024)S(1)} %get-tuple-element.2623, s32[2048]{0:T(1024)S(1)} %broadcast_clamp_fusion.16), kind=kCustom, calls=%fused_computation.4.clone.1 | custom fusion | bytes 24576 | tf_op jit(solution)/shard_map/while/body/eval_jaxpr/jit(_take)/gather | solution.py:41
  141.3 11.8 %gather_fusion.5 = s32[2048]{0:T(1024)S(1)} fusion(s32[4096]{0:T(1024)S(1)} %get-tuple-element.2622, s32[2048]{0:T(1024)S(1)} %broadcast_clamp_fusion.16), kind=kCustom, calls=%fused_computation.2.clone.1 | custom fusion | bytes 24576 | tf_op jit(solution)/shard_map/while/body/eval_jaxpr/jit(_take)/gather | solution.py:39
  167.5 11.8 %gather_fusion.3 = s32[2048]{0:T(1024)S(1)} fusion(s32[4096]{0:T(1024)S(1)} %get-tuple-element.2623, s32[2048]{0:T(1024)S(1)} %broadcast_clamp_fusion.16), kind=kCustom, calls=%fused_computation.4.clone.1 | custom fusion | bytes 24576 | tf_op jit(solution)/shard_map/while/body/eval_jaxpr/jit(_take)/gather | solution.py:41
  179.3 11.8 %gather_fusion.5 = s32[2048]{0:T(1024)S(1)} fusion(s32[4096]{0:T(1024)S(1)} %get-tuple-element.2622, s32[2048]{0:T(1024)S(1)} %broadcast_clamp_fusion.16), kind=kCustom, calls=%fused_computation.2.clone.1 | custom fusion | bytes 24576 | tf_op jit(solution)/shard_map/while/body/eval_jaxpr/jit(_take)/gather | solution.py:39
  207.4 96.3 %while.98 = (s32[]{:T(128)}, f32[16,128,128]{2,1,0:T(8,128)}, f32[16,128,128]{2,1,0:T(8,128)}, bf16[2,4,128,128]{3,2,1,0:T(8,128)(2,1)}, s32[2]{0:T(128)S(1)}, /...) while((s32[]{:T(128)}, f32[16,128,128]{2,1,0:T(8,128)}, ...), condition=%wide.region_13.16_spmd, body=%wide.region_7.15_spmd.sunk | while | flops 340863520 | bytes 28732392 | solution.py:183
  210.2 11.8 %gather_fusion.8 = s32[2048]{0:T(1024)S(1)} fusion(s32[4096]{0:T(1024)S(1)} %get-tuple-element.2679, s32[2048]{0:T(1024)S(1)} %broadcast_clamp_fusion.17), kind=kCustom, calls=%fused_computation.11.clone.1 | custom fusion | bytes 24576 | tf_op jit(solution)/shard_map/while/body/eval_jaxpr/jit(_take)/gather | solution.py:41
  222.0 11.8 %gather_fusion.10 = s32[2048]{0:T(1024)S(1)} fusion(s32[4096]{0:T(1024)S(1)} %get-tuple-element.2678, s32[2048]{0:T(1024)S(1)} %broadcast_clamp_fusion.17), kind=kCustom, calls=%fused_computation.9.clone.1 | custom fusion | bytes 24576 | tf_op jit(solution)/shard_map/while/body/eval_jaxpr/jit(_take)/gather | solution.py:39
  247.3 3.5 scatter_fusion
  258.5 11.8 %gather_fusion.8 = s32[2048]{0:T(1024)S(1)} fusion(s32[4096]{0:T(1024)S(1)} %get-tuple-element.2679, s32[2048]{0:T(1024)S(1)} %broadcast_clamp_fusion.17), kind=kCustom, calls=%fused_computation.11.clone.1 | custom fusion | bytes 24576 | tf_op jit(solution)/shard_map/while/body/eval_jaxpr/jit(_take)/gather | solution.py:41
  270.3 11.8 %gather_fusion.10 = s32[2048]{0:T(1024)S(1)} fusion(s32[4096]{0:T(1024)S(1)} %get-tuple-element.2678, s32[2048]{0:T(1024)S(1)} %broadcast_clamp_fusion.17), kind=kCustom, calls=%fused_computation.9.clone.1 | custom fusion | bytes 24576 | tf_op jit(solution)/shard_map/while/body/eval_jaxpr/jit(_take)/gather | solution.py:39
  303.7 75.6 %while.99 = (s32[]{:T(128)}, f32[2,4,128]{2,1,0:T(4,128)S(1)}, s32[2]{0:T(128)S(1)}, s32[]{:T(128)}, s32[32,2]{1,0:T(8,128)S(1)}, /*index=5*/s32[]{:T(128)}, s32...) while((s32[]{:T(128)}, f32[2,4,128]{2,1,0:T(4,128)S(1)}, ...), condition=%wide.region_20.23_spmd, body=%wide.region_14.22_spmd.sunk | while | flops 72624064 | bytes 4251355 | solution.py:127
  307.2 11.8 %gather_fusion.16 = s32[2048]{0:T(1024)S(1)} fusion(s32[4096]{0:T(1024)S(1)} %get-tuple-element.2521, s32[2048]{0:T(1024)S(1)} %broadcast_clamp_fusion.18), kind=kCustom, calls=%fused_computation.17.clone.1 | custom fusion | bytes 24576 | tf_op jit(solution)/shard_map/while/body/eval_jaxpr/jit(_take)/gather | solution.py:41
  319.0 11.8 %gather_fusion.18 = s32[2048]{0:T(1024)S(1)} fusion(s32[4096]{0:T(1024)S(1)} %get-tuple-element.2520, s32[2048]{0:T(1024)S(1)} %broadcast_clamp_fusion.18), kind=kCustom, calls=%fused_computation.15.clone.1 | custom fusion | bytes 24576 | tf_op jit(solution)/shard_map/while/body/eval_jaxpr/jit(_take)/gather | solution.py:39
  345.1 11.8 %gather_fusion.16 = s32[2048]{0:T(1024)S(1)} fusion(s32[4096]{0:T(1024)S(1)} %get-tuple-element.2521, s32[2048]{0:T(1024)S(1)} %broadcast_clamp_fusion.18), kind=kCustom, calls=%fused_computation.17.clone.1 | custom fusion | bytes 24576 | tf_op jit(solution)/shard_map/while/body/eval_jaxpr/jit(_take)/gather | solution.py:41
  356.8 11.8 %gather_fusion.18 = s32[2048]{0:T(1024)S(1)} fusion(s32[4096]{0:T(1024)S(1)} %get-tuple-element.2520, s32[2048]{0:T(1024)S(1)} %broadcast_clamp_fusion.18), kind=kCustom, calls=%fused_computation.15.clone.1 | custom fusion | bytes 24576 | tf_op jit(solution)/shard_map/while/body/eval_jaxpr/jit(_take)/gather | solution.py:39
  382.2 96.9 %while.100 = (s32[]{:T(128)}, f32[16,128,128]{2,1,0:T(8,128)}, f32[16,128,128]{2,1,0:T(8,128)}, bf16[2,4,128,128]{3,2,1,0:T(8,128)(2,1)}, s32[2]{0:T(128)S(1)}, ...) while((s32[]{:T(128)}, f32[16,128,128]{2,1,0:T(8,128)}, ...), condition=%wide.region_27.30_spmd, body=%wide.region_21.29_spmd.sunk | while | flops 340863520 | bytes 28732392 | solution.py:183
  385.3 11.8 %gather_fusion.21 = s32[2048]{0:T(1024)S(1)} fusion(s32[4096]{0:T(1024)S(1)} %get-tuple-element.2577, s32[2048]{0:T(1024)S(1)} %broadcast_clamp_fusion.19), kind=kCustom, calls=%fused_computation.24.clone.1 | custom fusion | bytes 24576 | tf_op jit(solution)/shard_map/while/body/eval_jaxpr/jit(_take)/gather | solution.py:41
  397.1 11.8 %gather_fusion.23 = s32[2048]{0:T(1024)S(1)} fusion(s32[4096]{0:T(1024)S(1)} %get-tuple-element.2576, s32[2048]{0:T(1024)S(1)} %broadcast_clamp_fusion.19), kind=kCustom, calls=%fused_computation.22.clone.1 | custom fusion | bytes 24576 | tf_op jit(solution)/shard_map/while/body/eval_jaxpr/jit(_take)/gather | solution.py:39
  422.5 3.5 scatter_fusion.2
  426.2 3.5 scatter_fusion.3
  433.8 11.8 %gather_fusion.21 = s32[2048]{0:T(1024)S(1)} fusion(s32[4096]{0:T(1024)S(1)} %get-tuple-element.2577, s32[2048]{0:T(1024)S(1)} %broadcast_clamp_fusion.19), kind=kCustom, calls=%fused_computation.24.clone.1 | custom fusion | bytes 24576 | tf_op jit(solution)/shard_map/while/body/eval_jaxpr/jit(_take)/gather | solution.py:41
  445.6 11.8 %gather_fusion.23 = s32[2048]{0:T(1024)S(1)} fusion(s32[4096]{0:T(1024)S(1)} %get-tuple-element.2576, s32[2048]{0:T(1024)S(1)} %broadcast_clamp_fusion.19), kind=kCustom, calls=%fused_computation.22.clone.1 | custom fusion | bytes 24576 | tf_op jit(solution)/shard_map/while/body/eval_jaxpr/jit(_take)/gather | solution.py:39
  479.1 75.6 %while.101 = (s32[]{:T(128)}, f32[2,4,128]{2,1,0:T(4,128)S(1)}, s32[2]{0:T(128)S(1)}, s32[]{:T(128)}, s32[32,2]{1,0:T(8,128)S(1)}, /*index=5*/s32[]{:T(128)}, s3...) while((s32[]{:T(128)}, f32[2,4,128]{2,1,0:T(4,128)S(1)}, ...), condition=%wide.region_34.37_spmd, body=%wide.region_28.36_spmd.sunk | while | flops 72624064 | bytes 4251355 | solution.py:127
  482.7 11.8 %gather_fusion.29 = s32[2048]{0:T(1024)S(1)} fusion(s32[4096]{0:T(1024)S(1)} %get-tuple-element.2419, s32[2048]{0:T(1024)S(1)} %broadcast_clamp_fusion.20), kind=kCustom, calls=%fused_computation.30.clone.1 | custom fusion | bytes 24576 | tf_op jit(solution)/shard_map/while/body/eval_jaxpr/jit(_take)/gather | solution.py:41
  494.5 11.8 %gather_fusion.31 = s32[2048]{0:T(1024)S(1)} fusion(s32[4096]{0:T(1024)S(1)} %get-tuple-element.2418, s32[2048]{0:T(1024)S(1)} %broadcast_clamp_fusion.20), kind=kCustom, calls=%fused_computation.28.clone.1 | custom fusion | bytes 24576 | tf_op jit(solution)/shard_map/while/body/eval_jaxpr/jit(_take)/gather | solution.py:39
  520.5 11.8 %gather_fusion.29 = s32[2048]{0:T(1024)S(1)} fusion(s32[4096]{0:T(1024)S(1)} %get-tuple-element.2419, s32[2048]{0:T(1024)S(1)} %broadcast_clamp_fusion.20), kind=kCustom, calls=%fused_computation.30.clone.1 | custom fusion | bytes 24576 | tf_op jit(solution)/shard_map/while/body/eval_jaxpr/jit(_take)/gather | solution.py:41
  532.3 11.8 %gather_fusion.31 = s32[2048]{0:T(1024)S(1)} fusion(s32[4096]{0:T(1024)S(1)} %get-tuple-element.2418, s32[2048]{0:T(1024)S(1)} %broadcast_clamp_fusion.20), kind=kCustom, calls=%fused_computation.28.clone.1 | custom fusion | bytes 24576 | tf_op jit(solution)/shard_map/while/body/eval_jaxpr/jit(_take)/gather | solution.py:39
  557.7 97.2 %while.102 = (s32[]{:T(128)}, f32[16,128,128]{2,1,0:T(8,128)}, f32[16,128,128]{2,1,0:T(8,128)}, bf16[2,4,128,128]{3,2,1,0:T(8,128)(2,1)}, s32[2]{0:T(128)S(1)}, ...) while((s32[]{:T(128)}, f32[16,128,128]{2,1,0:T(8,128)}, ...), condition=%wide.region_41.44_spmd, body=%wide.region_35.43_spmd.sunk | while | flops 340863520 | bytes 28732392 | solution.py:183
  560.9 11.8 %gather_fusion.34 = s32[2048]{0:T(1024)S(1)} fusion(s32[4096]{0:T(1024)S(1)} %get-tuple-element.2475, s32[2048]{0:T(1024)S(1)} %broadcast_clamp_fusion.21), kind=kCustom, calls=%fused_computation.37.clone.1 | custom fusion | bytes 24576 | tf_op jit(solution)/shard_map/while/body/eval_jaxpr/jit(_take)/gather | solution.py:41
  572.6 11.8 %gather_fusion.36 = s32[2048]{0:T(1024)S(1)} fusion(s32[4096]{0:T(1024)S(1)} %get-tuple-element.2474, s32[2048]{0:T(1024)S(1)} %broadcast_clamp_fusion.21), kind=kCustom, calls=%fused_computation.35.clone.1 | custom fusion | bytes 24576 | tf_op jit(solution)/shard_map/while/body/eval_jaxpr/jit(_take)/gather | solution.py:39
  598.0 3.6 scatter_fusion.4
  601.9 3.5 scatter_fusion.5
  609.5 11.8 %gather_fusion.34 = s32[2048]{0:T(1024)S(1)} fusion(s32[4096]{0:T(1024)S(1)} %get-tuple-element.2475, s32[2048]{0:T(1024)S(1)} %broadcast_clamp_fusion.21), kind=kCustom, calls=%fused_computation.37.clone.1 | custom fusion | bytes 24576 | tf_op jit(solution)/shard_map/while/body/eval_jaxpr/jit(_take)/gather | solution.py:41
  621.3 11.8 %gather_fusion.36 = s32[2048]{0:T(1024)S(1)} fusion(s32[4096]{0:T(1024)S(1)} %get-tuple-element.2474, s32[2048]{0:T(1024)S(1)} %broadcast_clamp_fusion.21), kind=kCustom, calls=%fused_computation.35.clone.1 | custom fusion | bytes 24576 | tf_op jit(solution)/shard_map/while/body/eval_jaxpr/jit(_take)/gather | solution.py:39
  655.0 75.6 %while.103 = (s32[]{:T(128)}, f32[2,4,128]{2,1,0:T(4,128)S(1)}, s32[2]{0:T(128)S(1)}, s32[]{:T(128)}, s32[32,2]{1,0:T(8,128)S(1)}, /*index=5*/s32[]{:T(128)}, s3...) while((s32[]{:T(128)}, f32[2,4,128]{2,1,0:T(4,128)S(1)}, ...), condition=%wide.region_48.51_spmd, body=%wide.region_42.50_spmd.sunk | while | flops 72624064 | bytes 4251355 | solution.py:127
  658.5 11.8 %gather_fusion.42 = s32[2048]{0:T(1024)S(1)} fusion(s32[4096]{0:T(1024)S(1)} %get-tuple-element.2317, s32[2048]{0:T(1024)S(1)} %broadcast_clamp_fusion.22), kind=kCustom, calls=%fused_computation.43.clone.1 | custom fusion | bytes 24576 | tf_op jit(solution)/shard_map/while/body/eval_jaxpr/jit(_take)/gather | solution.py:41
  670.3 11.8 %gather_fusion.44 = s32[2048]{0:T(1024)S(1)} fusion(s32[4096]{0:T(1024)S(1)} %get-tuple-element.2316, s32[2048]{0:T(1024)S(1)} %broadcast_clamp_fusion.22), kind=kCustom, calls=%fused_computation.41.clone.1 | custom fusion | bytes 24576 | tf_op jit(solution)/shard_map/while/body/eval_jaxpr/jit(_take)/gather | solution.py:39
  696.3 11.8 %gather_fusion.42 = s32[2048]{0:T(1024)S(1)} fusion(s32[4096]{0:T(1024)S(1)} %get-tuple-element.2317, s32[2048]{0:T(1024)S(1)} %broadcast_clamp_fusion.22), kind=kCustom, calls=%fused_computation.43.clone.1 | custom fusion | bytes 24576 | tf_op jit(solution)/shard_map/while/body/eval_jaxpr/jit(_take)/gather | solution.py:41
  708.1 11.8 %gather_fusion.44 = s32[2048]{0:T(1024)S(1)} fusion(s32[4096]{0:T(1024)S(1)} %get-tuple-element.2316, s32[2048]{0:T(1024)S(1)} %broadcast_clamp_fusion.22), kind=kCustom, calls=%fused_computation.41.clone.1 | custom fusion | bytes 24576 | tf_op jit(solution)/shard_map/while/body/eval_jaxpr/jit(_take)/gather | solution.py:39
  733.5 95.1 %while.104 = (s32[]{:T(128)}, f32[16,128,128]{2,1,0:T(8,128)}, f32[16,128,128]{2,1,0:T(8,128)}, bf16[2,4,128,128]{3,2,1,0:T(8,128)(2,1)}, s32[2]{0:T(128)S(1)}, ...) while((s32[]{:T(128)}, f32[16,128,128]{2,1,0:T(8,128)}, ...), condition=%wide.region_55.58_spmd, body=%wide.region_49.57_spmd.sunk | while | flops 340863520 | bytes 24538032 | solution.py:183
  736.7 11.8 %gather_fusion.47 = s32[2048]{0:T(1024)S(1)} fusion(s32[4096]{0:T(1024)S(1)} %get-tuple-element.2373, s32[2048]{0:T(1024)S(1)} %broadcast_clamp_fusion.23), kind=kCustom, calls=%fused_computation.50.clone.1 | custom fusion | bytes 24576 | tf_op jit(solution)/shard_map/while/body/eval_jaxpr/jit(_take)/gather | solution.py:41
  748.5 11.8 %gather_fusion.49 = s32[2048]{0:T(1024)S(1)} fusion(s32[4096]{0:T(1024)S(1)} %get-tuple-element.2372, s32[2048]{0:T(1024)S(1)} %broadcast_clamp_fusion.23), kind=kCustom, calls=%fused_computation.48.clone.1 | custom fusion | bytes 24576 | tf_op jit(solution)/shard_map/while/body/eval_jaxpr/jit(_take)/gather | solution.py:39
  773.0 3.5 scatter_fusion.6
  784.3 11.8 %gather_fusion.47 = s32[2048]{0:T(1024)S(1)} fusion(s32[4096]{0:T(1024)S(1)} %get-tuple-element.2373, s32[2048]{0:T(1024)S(1)} %broadcast_clamp_fusion.23), kind=kCustom, calls=%fused_computation.50.clone.1 | custom fusion | bytes 24576 | tf_op jit(solution)/shard_map/while/body/eval_jaxpr/jit(_take)/gather | solution.py:41
  796.1 11.8 %gather_fusion.49 = s32[2048]{0:T(1024)S(1)} fusion(s32[4096]{0:T(1024)S(1)} %get-tuple-element.2372, s32[2048]{0:T(1024)S(1)} %broadcast_clamp_fusion.23), kind=kCustom, calls=%fused_computation.48.clone.1 | custom fusion | bytes 24576 | tf_op jit(solution)/shard_map/while/body/eval_jaxpr/jit(_take)/gather | solution.py:39
  841.0 3.9 all-to-all-start.5
  844.9 40.1 %collective-permute-done.3 = f32[1024,512]{1,0:T(8,128)S(1)} collective-permute-done((f32[1024,512]{1,0:T(8,128)}, f32[1024,512]{1,0:T(8,128)S(1)}, u32[]{:S(2)}, u32[]{:S(2)}) %collective-permute-start.3) | collective-permute-done | bytes 2097184 | tf_op jit(solution)/shard_map/ppermute | solution.py:18
  887.9 3.9 all-to-all-start.7
  891.7 37.0 %collective-permute-done.2 = f32[1024,512]{1,0:T(8,128)} collective-permute-done((f32[1024,512]{1,0:T(8,128)}, f32[1024,512]{1,0:T(8,128)}, u32[]{:S(2)}, u32[]{:S(2)}) %collective-permute-start.2) | collective-permute-done | bytes 2097184 | tf_op jit(solution)/shard_map/ppermute | solution.py:18
  928.7 3.6 fusion.117
  932.3 4.5 all-to-all-start.6
  943.1 9.0 all-to-all-done.6
  (797 shorter events, 323.9 us)
Async XLA Ops:
  0.6 5.3 copy-start
  0.6 10.1 %all-to-all-start.4 = ((f32[128,8,4]{0,2,1:T(4,128)}), f32[128,8,4]{0,2,1:T(4,128)S(1)}, u32[]{:S(2)}, u32[]{:S(2)}) async-start(f32[128,8,4]{0,2,1:T(4,128)} %bitcast.921), calls=%async_computation.4 | async-start | bytes 32768 | tf_op jit(solution)/shard_map/all_to_all | solution.py:220
  6.3 8.0 copy-start.30
  10.7 18.9 %all-to-all-start = ((bf16[128,8,512]{2,0,1:T(8,128)(2,1)}), bf16[128,8,512]{2,0,1:T(8,128)(2,1)S(1)}, u32[]{:S(2)}, u32[]{:S(2)}) async-start(bf16[128,8,512]{2,0,1:T(8,128)(2,1)} %all_to_all.102), calls=%async_computation | async-start | bytes 2097152 | tf_op jit(solution)/shard_map/all_to_all | solution.py:209
  14.3 18.9 %copy-start.44 = (bf16[128,1024]{1,0:T(8,128)(2,1)S(1)}, bf16[128,1024]{1,0:T(8,128)(2,1)}, u32[]{:S(2)}) copy-start(bf16[128,1024]{1,0:T(8,128)(2,1)} %param.30) | copy-start | bytes 786436
  29.6 3.6 copy-start.25
  29.6 18.9 %all-to-all-start.1 = ((bf16[128,8,512]{2,0,1:T(8,128)(2,1)}), bf16[128,8,512]{2,0,1:T(8,128)(2,1)S(1)}, u32[]{:S(2)}, u32[]{:S(2)}) async-start(bf16[128,8,512]{2,0,1:T(8,128)(2,1)} %bitcast.478), calls=%async_computation.1 | async-start | bytes 2097152 | tf_op jit(solution)/shard_map/all_to_all | solution.py:207
  33.5 18.6 %copy-start.47 = (s32[8,32,2]{1,2,0:T(2,128)S(1)}, s32[8,32,2]{1,2,0:T(2,128)}, u32[]{:S(2)}) copy-start(s32[8,32,2]{1,2,0:T(2,128)} %param.35) | copy-start | bytes 6148
  34.8 17.5 %copy-start.31 = (bf16[128,4096]{1,0:T(8,128)(2,1)S(1)}, bf16[128,4096]{1,0:T(8,128)(2,1)}, u32[]{:S(2)}) copy-start(bf16[128,4096]{1,0:T(8,128)(2,1)} %param.31) | copy-start | bytes 3145732
  34.8 20.0 %copy-start.27 = (s32[64]{0:T(128)S(1)}, s32[64]{0:T(128)}, u32[]{:S(2)}) copy-start(s32[64]{0:T(128)} %param.34) | copy-start | bytes 772
  48.5 18.9 %all-to-all-start.2 = ((bf16[128,8,512]{2,0,1:T(8,128)(2,1)}), bf16[128,8,512]{2,0,1:T(8,128)(2,1)S(1)}, u32[]{:S(2)}, u32[]{:S(2)}) async-start(bf16[128,8,512]{2,0,1:T(8,128)(2,1)} %all_to_all.110), calls=%async_computation.2 | async-start | bytes 2097152 | tf_op jit(solution)/shard_map/all_to_all | solution.py:212
  52.3 23.9 %copy-start.2 = (s32[4096]{0:T(1024)S(1)}, s32[4096]{0:T(1024)}, u32[]{:S(2)}) copy-start(s32[4096]{0:T(1024)} %param.33) | copy-start | bytes 49156
  67.4 54.3 %all-to-all-start.3 = ((bf16[128,8,512]{2,0,1:T(8,128)(2,1)}), bf16[128,8,512]{2,0,1:T(8,128)(2,1)S(1)}, u32[]{:S(2)}, u32[]{:S(2)}) async-start(bf16[128,8,512]{2,0,1:T(8,128)(2,1)} %bitcast.477), calls=%async_computation.3 | async-start | bytes 2097152 | tf_op jit(solution)/shard_map/all_to_all | solution.py:208
  71.7 51.2 %collective-permute-start = (bf16[1024,512]{1,0:T(8,128)(2,1)}, bf16[1024,512]{1,0:T(8,128)(2,1)}, u32[]{:S(2)}, u32[]{:S(2)}) collective-permute-start(bf16[1024,512]{1,0:T(8,128)(2,1)} %bitcast.842), channel_id=1, source_target_pairs={{0,8},{8,16},{16,24},{1,9},{9,17},{17,25},{2,10},{10,18},{18,26},{... | collective-permute-start | bytes 3145736 | tf_op jit(solution)/shard_map/ppermute | solution.py:18
  116.7 85.1 %collective-permute-start.1 = (bf16[1024,512]{1,0:T(8,128)(2,1)S(1)}, bf16[1024,512]{1,0:T(8,128)(2,1)}, u32[]{:S(2)}, u32[]{:S(2)}) collective-permute-start(bf16[1024,512]{1,0:T(8,128)(2,1)S(1)} %bitcast.840), channel_id=1, source_target_pairs={{0,8},{8,16},{16,24},{1,9},{9,17},{17,25},{2,10},{10,18},{18,26},{... | collective-permute-start | bytes 3145736 | tf_op jit(solution)/shard_map/ppermute | solution.py:18
  234.6 8.2 copy-start.17
  251.0 3.5 copy-start.6
  251.0 3.5 copy-start.18
  251.1 3.4 copy-start.35
  282.9 8.2 copy-start.17
  299.2 3.3 copy-start.6
  299.2 3.3 copy-start.18
  299.2 3.3 copy-start.35
  382.2 96.9 %copy-start.4 = (bf16[2048,128]{1,0:T(8,128)(2,1)S(1)}, bf16[2048,128]{1,0:T(8,128)(2,1)}, u32[]{:S(2)}) copy-start(bf16[2048,128]{1,0:T(8,128)(2,1)} %get-tuple-element.1401) | copy-start | bytes 1572868
  382.2 96.9 %copy-start.29 = (s32[32,2]{1,0:T(8,128)S(1)}, s32[32,2]{1,0:T(8,128)}, u32[]{:S(2)}) copy-start(s32[32,2]{1,0:T(8,128)} %copy.135) | copy-start | bytes 772
  409.7 8.3 copy-start.19
  426.2 3.5 copy-start.8
  426.2 3.5 copy-start.20
  426.2 3.5 copy-start.38
  458.2 8.3 copy-start.19
  474.6 3.4 copy-start.8
  474.6 3.4 copy-start.20
  474.6 3.4 copy-start.38
  554.7 3.0 copy-start.46
  557.7 97.2 %copy-start.3 = (bf16[2048,128]{1,0:T(8,128)(2,1)S(1)}, bf16[2048,128]{1,0:T(8,128)(2,1)}, u32[]{:S(2)}) copy-start(bf16[2048,128]{1,0:T(8,128)(2,1)} %get-tuple-element.1400) | copy-start | bytes 1572868
  557.7 97.2 %copy-start.28 = (s32[32,2]{1,0:T(8,128)S(1)}, s32[32,2]{1,0:T(8,128)}, u32[]{:S(2)}) copy-start(s32[32,2]{1,0:T(8,128)} %copy.137) | copy-start | bytes 772
  585.2 8.3 copy-start.21
  601.9 3.5 copy-start.10
  601.9 3.5 copy-start.22
  601.9 3.5 copy-start.41
  633.9 8.3 copy-start.21
  650.4 3.4 copy-start.10
  650.4 3.4 copy-start.22
  650.4 3.4 copy-start.41
  761.0 8.2 copy-start.23
  776.8 3.4 copy-start.24
  776.8 3.4 copy-start.32
  808.6 8.2 copy-start.23
  824.1 3.3 copy-start.24
  824.2 3.3 copy-start.32
  831.1 3.1 copy-start.16
  831.1 4.5 copy-start.11
  831.1 4.5 copy-start.12
  831.1 4.5 copy-start.13
  831.1 4.5 copy-start.14
  834.2 50.8 %collective-permute-start.3 = (f32[1024,512]{1,0:T(8,128)}, f32[1024,512]{1,0:T(8,128)S(1)}, u32[]{:S(2)}, u32[]{:S(2)}) collective-permute-start(f32[1024,512]{1,0:T(8,128)} %slice.301), channel_id=1, source_target_pairs={{8,0},{16,8},{24,16},{9,1},{17,9},{25,17},{10,2},{18,10},{26,18},{... | collective-permute-start | bytes 6291464 | tf_op jit(solution)/shard_map/ppermute | solution.py:18
  836.0 3.9 copy-start.34
  836.0 3.9 copy-start.37
  836.0 3.9 copy-start.40
  836.0 3.9 copy-start.43
  838.5 90.2 %collective-permute-start.2 = (f32[1024,512]{1,0:T(8,128)}, f32[1024,512]{1,0:T(8,128)}, u32[]{:S(2)}, u32[]{:S(2)}) collective-permute-start(f32[1024,512]{1,0:T(8,128)} %slice.299), channel_id=1, source_target_pairs={{8,0},{16,8},{24,16},{9,1},{17,9},{25,17},{10,2},{18,10},{26,18},{... | collective-permute-start | bytes 6291464 | tf_op jit(solution)/shard_map/ppermute | solution.py:18
  841.0 46.9 %all-to-all-start.5 = ((bf16[8,128,512]{2,1,0:T(8,128)(2,1)}), bf16[8,128,512]{2,1,0:T(8,128)(2,1)S(1)}, u32[]{:S(2)}, u32[]{:S(2)}) async-start(bf16[8,128,512]{2,1,0:T(8,128)(2,1)} %pad_maximum_fusion.2), calls=%async_computation.5 | async-start | bytes 2097152 | tf_op jit(solution)/shard_map/all_to_all | solution.py:281
  887.9 44.4 %all-to-all-start.7 = ((bf16[8,128,512]{2,1,0:T(8,128)(2,1)}), bf16[8,128,512]{2,1,0:T(8,128)(2,1)S(1)}, u32[]{:S(2)}, u32[]{:S(2)}) async-start(bf16[8,128,512]{2,1,0:T(8,128)(2,1)} %bitcast.283), calls=%async_computation.7 | async-start | bytes 2097152 | tf_op jit(solution)/shard_map/all_to_all | solution.py:287
  932.3 19.8 %all-to-all-start.6 = ((bf16[8,128,512]{2,1,0:T(8,128)(2,1)}), bf16[8,128,512]{2,1,0:T(8,128)(2,1)S(1)}, u32[]{:S(2)}, u32[]{:S(2)}) async-start(bf16[8,128,512]{2,1,0:T(8,128)(2,1)} %bitcast.276), calls=%async_computation.6 | async-start | bytes 2097152 | tf_op jit(solution)/shard_map/all_to_all | solution.py:284
  (18 other events, 20.4 us)
where the time goes:
time: 961 us; the launch traced here: 955 us
  local copies, waits for them, and re-layouts  590 us (61%)
  other arithmetic  138 us (14%)
  waiting for transfers between devices  128 us (13%)
  starting transfers between devices  43 us (4%)
  matrix products  31.3 us (3%)
  loops' own time  23.7 us (2%)
    gather x16, local copies, waits for them, and re-layouts, allowed_tiles(): key_doc = jnp.take(doc_ids, key_pos, mode='clip')  189 us
    gather x16, local copies, waits for them, and re-layouts, allowed_tiles(): key_lang = jnp.take(position_lang, key_pos, mode='clip')  188 us
    ppermute x4, waiting for transfers between devices, from_behind(): return lax.ppermute(block, axis, route)  77 us
    gather x16, local copies, waits for them, and re-layouts, allowed_tiles(): query_doc = jnp.take(doc_ids, query_pos, mode='clip')  50.3 us
    gather x16, local copies, waits for them, and re-layouts, allowed_tiles(): query_lang = jnp.take(position_lang, query_pos, mode='clip')  50.2 us
    gather x1, other arithmetic, shards(): position_lang = jnp.take(doc_lang, doc_ids, mode='clip')  39.9 us
    scatter-add x8, other arithmetic, scan_step(): key_sum = key_sum.at[flat_slot].add(grad_key.reshape(-1, BLOCK, DH))  27.3 us
    scatter-add x8, other arithmetic, scan_step(): value_sum = value_sum.at[flat_slot].add(grad_value.reshape(-1, BLOCK, DH))  27.2 us
  transfers between devices with their start and end apart: 12, of which 7 were waited for; matrix products, arithmetic and copies ran while one was open for 15% of the time, Pallas kernels for 0%

commit v1 on v0

v1 whole, which is shorter than its diff:
```python
import functools

import jax
import jax.numpy as jnp
from jax import lax
from jax.experimental import pallas as pl
from jax.experimental.pallas import tpu as pltpu
from jax.sharding import PartitionSpec as P

DH = 128
BLOCK = 128
LANGS = 4
MASKED = -1e30
MESH = pl.DeviceIdType.MESH
VMEM_LIMIT = 56 * 1024 * 1024


def greet(b, u, n_blk, n_uly):
    barrier = pltpu.get_barrier_semaphore()
    for p in range(1, n_uly):
        pl.semaphore_signal(
            barrier, inc=1, device_id=(b, lax.rem(u + p, n_uly)), device_id_type=MESH
        )

    @pl.when(b > 0)
    def _():
        pl.semaphore_signal(barrier, inc=1, device_id=(b - 1, u), device_id_type=MESH)

    @pl.when(b < n_blk - 1)
    def _():
        pl.semaphore_signal(barrier, inc=1, device_id=(b + 1, u), device_id_type=MESH)

    ends = jnp.where(b > 0, 1, 0) + jnp.where(b < n_blk - 1, 1, 0)
    pl.semaphore_wait(barrier, n_uly - 1 + ends)


def aligned(start, size):
    return pl.ds(pl.multiple_of(start, size), size)


def gather_kernel(
    n_blk,
    n_uly,
    heads_here,
    repeat_count,
    q_ref,
    do_ref,
    k_ref,
    v_ref,
    dl_ref,
    qo_ref,
    doo_ref,
    kw_ref,
    vw_ref,
    dlo_ref,
    send_sem,
    recv_sem,
    z_send,
    z_recv,
    local_sem,
):
    b, u = lax.axis_index("blk"), lax.axis_index("uly")
    tok = q_ref.shape[0]
    rows = tok * n_uly
    width = heads_here * DH
    mine = aligned(u * tok, tok)
    window_mine = aligned(rows + u * tok, tok)

    def pieces(peer):
        group = lax.div(peer * heads_here, repeat_count)
        kv_cols = aligned(group * DH, DH)
        q_cols = aligned(peer * width, width)
        return (
            (k_ref.at[:, kv_cols], kw_ref.at[window_mine, :]),
            (v_ref.at[:, kv_cols], vw_ref.at[window_mine, :]),
            (dl_ref.at[peer], dlo_ref.at[u]),
            (q_ref.at[:, q_cols], qo_ref.at[mine, :]),
            (do_ref.at[:, q_cols], doo_ref.at[mine, :]),
        )

    def remote(kind, p):
        peer = lax.rem(u + p, n_uly)
        src, dst = pieces(peer)[kind]
        return pltpu.make_async_remote_copy(
            src_ref=src,
            dst_ref=dst,
            send_sem=send_sem.at[kind, p],
            recv_sem=recv_sem.at[kind, p],
            device_id=(b, peer),
            device_id_type=MESH,
        )

    def local(kind):
        src, dst = pieces(u)[kind]
        return pltpu.make_async_copy(src, dst, local_sem.at[kind])

    def forward(kind):
        ref = (kw_ref, vw_ref)[kind]
        return pltpu.make_async_remote_copy(
            src_ref=ref.at[pl.ds(rows, rows), :],
            dst_ref=ref.at[pl.ds(0, rows), :],
            send_sem=z_send.at[kind],
            recv_sem=z_recv.at[kind],
            device_id=(lax.rem(b + 1, n_blk), u),
            device_id_type=MESH,
        )

    for kind in range(5):
        local(kind).start()
    greet(b, u, n_blk, n_uly)
    for kind in (0, 1):
        for p in range(1, n_uly):
            remote(kind, p).start()
    for p in range(1, n_uly):
        for kind in (2, 3, 4):
            remote(kind, p).start()
    for kind in (0, 1):
        local(kind).wait()
        for p in range(1, n_uly):
            remote(kind, p).wait_recv()

        @pl.when(b < n_blk - 1)
        def _():
            forward(kind).start()

    for kind in (2, 3, 4):
        local(kind).wait()
        for p in range(1, n_uly):
            remote(kind, p).wait_recv()
    for kind in range(5):
        for p in range(1, n_uly):
            remote(kind, p).wait_send()
    for kind in (0, 1):

        @pl.when(b < n_blk - 1)
        def _():
            forward(kind).wait_send()

        @pl.when(b > 0)
        def _():
            forward(kind).wait_recv()


def gathered(queries, grad_out, keys, values, delta_rows, n_blk, n_uly, repeat_count):
    tok_count, full_width = queries.shape
    rows = tok_count * n_uly
    width = full_width // n_uly
    heads_here = width // DH
    anywhere = pl.BlockSpec(memory_space=pl.ANY)
    bf16 = jnp.bfloat16
    return pl.pallas_call(
        functools.partial(gather_kernel, n_blk, n_uly, heads_here, repeat_count),
        out_shape=(
            jax.ShapeDtypeStruct((rows, width), bf16),
            jax.ShapeDtypeStruct((rows, width), bf16),
            jax.ShapeDtypeStruct((2 * rows, DH), bf16),
            jax.ShapeDtypeStruct((2 * rows, DH), bf16),
            jax.ShapeDtypeStruct((n_uly, heads_here, tok_count), jnp.float32),
        ),
        in_specs=[anywhere] * 5,
        out_specs=(anywhere,) * 5,
        scratch_shapes=[
            pltpu.SemaphoreType.DMA((5, n_uly)),
            pltpu.SemaphoreType.DMA((5, n_uly)),
            pltpu.SemaphoreType.DMA((2,)),
            pltpu.SemaphoreType.DMA((2,)),
            pltpu.SemaphoreType.DMA((5,)),
        ],
        compiler_params=pltpu.CompilerParams(collective_id=0, has_side_effects=True),
        name="gather_heads",
    )(queries, grad_out, keys, values, delta_rows)


def grads_kernel(
    tiles_here,
    tile_total,
    list_count,
    heads_here,
    repeat_count,
    list_ref,
    q_ref,
    do_ref,
    dl_ref,
    kw_ref,
    vw_ref,
    code_ref,
    dq_ref,
    back_ref,
    own_ref,
    key_codes,
    acc,
):
    a = pl.program_id(0)
    b, u = lax.axis_index("blk"), lax.axis_index("uly")
    rows = tiles_here * BLOCK
    scaling = float(DH) ** (-0.5)

    @pl.when(a == 0)
    def _():
        acc[...] = jnp.zeros_like(acc)

        @pl.loop(0, 2 * tiles_here)
        def _(t):
            row = jnp.broadcast_to(code_ref[pl.ds(t, 1), :], (BLOCK, BLOCK))
            key_codes[t] = row.T

    group = lax.div(u * heads_here, repeat_count)
    tile = b * tiles_here + a
    base = (group * tile_total + tile) * list_count
    listed = [list_ref[base + l] for l in range(list_count)]
    cands = [tile - 1, tile] + listed
    own_slot = tiles_here + a
    window_first = (b - 1) * tiles_here
    query_code = code_ref[pl.ds(own_slot, 1), :]
    query_lang = query_code & (LANGS - 1)
    gap = lax.broadcasted_iota(jnp.int32, (BLOCK, BLOCK), 0) - lax.broadcasted_iota(
        jnp.int32, (BLOCK, BLOCK), 1
    )
    slots = []
    biases = []
    for c, cand in enumerate(cands):
        usable = cand >= 0
        for other in cands[: c if c >= 2 else 0]:
            usable = usable & (cand != other)
        marked = cand == listed[0]
        for other in listed[1:]:
            marked = marked | (cand == other)
        slot = jnp.clip(cand - window_first, 0, 2 * tiles_here - 1)
        slot = jnp.where(usable, slot, own_slot)
        limit = jnp.where(usable, (tile - cand) * BLOCK, -2 * BLOCK)
        seen_lang = jnp.where(marked, query_lang, -1)
        key_code = key_codes[slot]
        allowed = (gap <= limit) & (
            (key_code == query_code) | ((key_code & (LANGS - 1)) == seen_lang)
        )
        slots.append(aligned(slot * BLOCK, BLOCK))
        biases.append(jnp.where(allowed, 0.0, MASKED))

    def stacked(ref):
        return jnp.concatenate([ref[:, h * DH : (h + 1) * DH] for h in range(heads_here)], axis=0)

    across = (((1,), (1,)), ((), ()))
    f32 = jnp.float32
    bias = jnp.concatenate(biases, axis=0)
    bias = jnp.concatenate([bias] * heads_here, axis=1)
    key_part = jnp.concatenate([kw_ref[s, :] for s in slots], axis=0)
    value_part = jnp.concatenate([vw_ref[s, :] for s in slots], axis=0)
    query_part = stacked(q_ref)
    dout_part = stacked(do_ref)
    delta = jnp.concatenate([dl_ref[0, h : h + 1, :] for h in range(heads_here)], axis=1)
    scores = lax.dot_general(key_part, query_part, across, preferred_element_type=f32)
    scores = scores * scaling + bias
    top = jnp.max(scores, axis=0, keepdims=True)
    raised = jnp.exp(scores - top)
    weights = raised * (1.0 / jnp.sum(raised, axis=0, keepdims=True))
    grad_weights = lax.dot_general(value_part, dout_part, across, preferred_element_type=f32)
    grad_scores = (weights * (grad_weights - delta)).astype(jnp.bfloat16)
    grad_value = jnp.dot(weights.astype(jnp.bfloat16), dout_part, preferred_element_type=f32)
    grad_key = scaling * jnp.dot(grad_scores, query_part, preferred_element_type=f32)
    grad_query = scaling * lax.dot_general(
        grad_scores, key_part, (((0,), (0,)), ((), ())), preferred_element_type=f32
    )
    for h in range(heads_here):
        dq_ref[:, h * DH : (h + 1) * DH] = grad_query[h * BLOCK : (h + 1) * BLOCK].astype(
            dq_ref.dtype
        )
    for c, s in enumerate(slots):
        acc[0, s, :] += grad_key[c * BLOCK : (c + 1) * BLOCK]
        acc[1, s, :] += grad_value[c * BLOCK : (c + 1) * BLOCK]

    @pl.when(a == tiles_here - 1)
    def _():
        back_ref[...] = acc[:, :rows, :].astype(back_ref.dtype)
        own_ref[...] = acc[:, rows:, :]


def grads(lists, query_heads, dout_heads, delta_heads, key_window, value_window, codes, sizes):
    tiles_here, tile_total, list_count, heads_here, repeat_count = sizes
    rows, width = query_heads.shape
    whole = pl.BlockSpec(memory_space=pltpu.VMEM)
    tile_spec = pl.BlockSpec((BLOCK, width), lambda a: (a, 0))
    flops = 5 * 2 * DH * rows * heads_here * (2 + list_count) * BLOCK
    return pl.pallas_call(
        functools.partial(grads_kernel, *sizes),
        grid=(tiles_here,),
        out_shape=(
            jax.ShapeDtypeStruct((rows, width), jnp.bfloat16),
            jax.ShapeDtypeStruct((2, rows, DH), jnp.bfloat16),
            jax.ShapeDtypeStruct((2, rows, DH), jnp.float32),
        ),
        in_specs=[
            pl.BlockSpec(memory_space=pltpu.SMEM),
            tile_spec,
            tile_spec,
            pl.BlockSpec((1, heads_here, BLOCK), lambda a: (a, 0, 0)),
            whole,
            whole,
            whole,
        ],
        out_specs=(
            tile_spec,
            pl.BlockSpec((2, rows, DH), lambda a: (0, 0, 0)),
            pl.BlockSpec((2, rows, DH), lambda a: (0, 0, 0)),
        ),
        scratch_shapes=[
            pltpu.VMEM((2 * tiles_here, BLOCK, BLOCK), jnp.int32),
            pltpu.VMEM((2, 2 * rows, DH), jnp.float32),
        ],
        compiler_params=pltpu.CompilerParams(
            dimension_semantics=("arbitrary",), vmem_limit_bytes=VMEM_LIMIT
        ),
        cost_estimate=pl.CostEstimate(
            flops=flops, bytes_accessed=12 * rows * width, transcendentals=flops // (10 * DH)
        ),
        name="tile_grads",
    )(lists, query_heads, dout_heads, delta_heads, key_window, value_window, codes)


def scatter_kernel(
    n_blk,
    n_uly,
    heads_here,
    repeat_count,
    dqh_ref,
    back_ref,
    own_ref,
    dq_ref,
    dk_ref,
    dv_ref,
    returned,
    total,
    landing,
    send_sem,
    recv_sem,
    z_send,
    z_recv,
    local_sem,
):
    b, u = lax.axis_index("blk"), lax.axis_index("uly")
    tok = dq_ref.shape[0]
    width = heads_here * DH
    copies = repeat_count // heads_here
    direct = copies == 1
    my_cols = aligned(u * width, width)
    my_group = aligned(u * DH, DH)

    def pieces(peer):
        theirs = aligned(peer * tok, tok)
        if direct:
            ends = (dk_ref.at[:, my_group], dv_ref.at[:, my_group])
        else:
            ends = (landing.at[0, u], landing.at[1, u])
        return (
            (total.at[0, theirs, :], ends[0]),
            (total.at[1, theirs, :], ends[1]),
            (dqh_ref.at[theirs, :], dq_ref.at[:, my_cols]),
        )

    def remote(kind, p):
        peer = lax.rem(u + p, n_uly)
        src, dst = pieces(peer)[kind]
        return pltpu.make_async_remote_copy(
            src_ref=src,
            dst_ref=dst,
            send_sem=send_sem.at[kind, p],
            recv_sem=recv_sem.at[kind, p],
            device_id=(b, peer),
            device_id_type=MESH,
        )

    def local(kind):
        src, dst = pieces(u)[kind]
        return pltpu.make_async_copy(src, dst, local_sem.at[kind])

    def backward(kind):
        return pltpu.make_async_remote_copy(
            src_ref=back_ref.at[kind],
            dst_ref=returned.at[kind],
            send_sem=z_send.at[kind],
            recv_sem=z_recv.at[kind],
            device_id=(lax.rem(b + n_blk - 1, n_blk), u),
            device_id_type=MESH,
        )

    local(2).start()
    greet(b, u, n_blk, n_uly)

    for kind in (0, 1):

        @pl.when(b > 0)
        def _():
            backward(kind).start()

    for p in range(1, n_uly):
        remote(2, p).start()

    for kind in (0, 1):

        @pl.when(b < n_blk - 1)
        def _():
            backward(kind).wait_recv()
            total[kind] = (own_ref[kind] + returned[kind].astype(jnp.float32)).astype(total.dtype)

        @pl.when(b == n_blk - 1)
        def _():
            total[kind] = own_ref[kind].astype(total.dtype)

        local(kind).start()
        for p in range(1, n_uly):
            remote(kind, p).start()

    for kind in (0, 1, 2):
        local(kind).wait()
        for p in range(1, n_uly):
            remote(kind, p).wait_recv()
    if not direct:
        for kind, out in ((0, dk_ref), (1, dv_ref)):
            for g in range(n_uly // copies):
                summed = landing[kind, g * copies].astype(jnp.float32)
                for r in range(1, copies):
                    summed = summed + landing[kind, g * copies + r].astype(jnp.float32)
                out[:, g * DH : (g + 1) * DH] = summed.astype(out.dtype)
    for kind in (0, 1, 2):
        for p in range(1, n_uly):
            remote(kind, p).wait_send()
    for kind in (0, 1):

        @pl.when(b > 0)
        def _():
            backward(kind).wait_send()


def scattered(dq_heads, back, own, n_blk, n_uly, repeat_count):
    rows, width = dq_heads.shape
    tok_count = rows // n_uly
    heads_here = width // DH
    copies = repeat_count // heads_here
    groups_all = n_uly // copies
    bf16 = jnp.bfloat16
    anywhere = pl.BlockSpec(memory_space=pl.ANY)
    in_vmem = pl.BlockSpec(memory_space=pltpu.VMEM)
    landing_count = n_uly if copies > 1 else 1
    kv_spec = in_vmem if copies > 1 else anywhere
    return pl.pallas_call(
        functools.partial(scatter_kernel, n_blk, n_uly, heads_here, repeat_count),
        out_shape=(
            jax.ShapeDtypeStruct((tok_count, width * n_uly), bf16),
            jax.ShapeDtypeStruct((tok_count, groups_all * DH), bf16),
            jax.ShapeDtypeStruct((tok_count, groups_all * DH), bf16),
        ),
        in_specs=[anywhere, anywhere, in_vmem],
        out_specs=(anywhere, kv_spec, kv_spec),
        scratch_shapes=[
            pltpu.VMEM((2, rows, DH), bf16),
            pltpu.VMEM((2, rows, DH), bf16),
            pltpu.VMEM((2, landing_count, tok_count, DH), bf16),
            pltpu.SemaphoreType.DMA((3, n_uly)),
            pltpu.SemaphoreType.DMA((3, n_uly)),
            pltpu.SemaphoreType.DMA((2,)),
            pltpu.SemaphoreType.DMA((2,)),
            pltpu.SemaphoreType.DMA((3,)),
        ],
        compiler_params=pltpu.CompilerParams(
            collective_id=1, has_side_effects=True, vmem_limit_bytes=VMEM_LIMIT
        ),
        name="scatter_tokens",
    )(dq_heads, back, own)


def window_codes(doc_ids, doc_lang, row_count):
    block_index = lax.axis_index("blk")
    earlier = lax.dynamic_slice_in_dim(
        doc_ids, jnp.maximum(block_index - 1, 0) * row_count, row_count
    )
    here = lax.dynamic_slice_in_dim(doc_ids, block_index * row_count, row_count)
    docs = jnp.concatenate([earlier, here]).reshape(-1, BLOCK)
    numbers = jnp.arange(doc_lang.shape[0], dtype=jnp.int32)
    hit = docs[None] == numbers[:, None, None]
    lang = jnp.sum(jnp.where(hit, doc_lang[:, None, None], 0), axis=0)
    return docs * LANGS + lang


def shards(queries, keys, values, grad_out, row_delta, doc_ids, doc_lang, tile_list):
    tok_count, full_width = queries.shape
    heads_all = full_width // DH
    groups_all = keys.shape[1] // DH
    repeat_count = heads_all // groups_all
    n_uly = lax.axis_size("uly")
    n_blk = lax.axis_size("blk")
    heads_here = heads_all // n_uly
    row_count = tok_count * n_uly
    sizes = (
        row_count // BLOCK,
        tile_list.shape[1],
        tile_list.shape[2],
        heads_here,
        repeat_count,
    )
    delta_rows = row_delta.T.reshape(n_uly, heads_here, tok_count)
    codes = window_codes(doc_ids, doc_lang, row_count)
    query_heads, dout_heads, key_window, value_window, delta_heads = gathered(
        queries, grad_out, keys, values, delta_rows, n_blk, n_uly, repeat_count
    )
    dq_heads, back, own = grads(
        tile_list.reshape(-1),
        query_heads,
        dout_heads,
        delta_heads,
        key_window,
        value_window,
        codes,
        sizes,
    )
    return scattered(dq_heads, back, own, n_blk, n_uly, repeat_count)


def solution(mesh):
    placed = (
        P(("blk", "uly"), None),
        P(("blk", "uly"), None),
        P(("blk", "uly"), None),
        P(("blk", "uly"), None),
        P(("blk", "uly"), None),
        P(),
        P(),
        P(),
    )
    return jax.shard_map(
        shards,
        mesh=mesh,
        in_specs=placed,
        out_specs=(P(("blk", "uly"), None), P(("blk", "uly"), None), P(("blk", "uly"), None)),
        check_vma=False,
    )
```

time: 961 us -> 79.4 us (0.08)
  local copies, waits for them, and re-layouts: 590 us -> 6.37 us
  other arithmetic: 138 us -> 0.74 us
  waiting for transfers between devices: 128 us -> 0 us
  Pallas kernels: 0 us -> 71.2 us
  starting transfers between devices: 43 us -> 0 us
  matrix products: 31.3 us -> 0 us
  loops' own time: 23.7 us -> 0 us
    gather x124 -> x0, local copies, waits for them, and re-layouts: 515 us -> none  [the longest x16 189 us: allowed_tiles(): key_doc = jnp.take(doc_ids, key_pos, mode='clip')]
    ppermute x4 -> x0, waiting for transfers between devices: 77 us -> none  [from_behind(): return lax.ppermute(block, axis, route)]
    pallas_call x0 -> x3, Pallas kernels: none -> 71.2 us  [the longest x1 33.8 us: gathered(): pl.pallas_call(functools.partial(gather_kernel, n_blk, n_uly, heads_here,...]
    scatter-add x16 -> x0, other arithmetic: 54.5 us -> none  [the longest x8 27.3 us: scan_step(): key_sum = key_sum.at[flat_slot].add(grad_key.reshape(-1, BLOCK, DH))]
    all_to_all x8 -> x0, waiting for transfers between devices: 50.6 us -> none  [the longest x1 14.2 us: shards(): lax.all_to_all(widened(keys, groups_all, repeat_count), 'uly', split_axis...]
    gather x65 -> x0, other arithmetic: 40.4 us -> none  [the longest x1 39.9 us: shards(): position_lang = jnp.take(doc_lang, doc_ids, mode='clip')]
    all_to_all x8 -> x0, starting transfers between devices: 31.8 us -> none  [the longest x1 5.31 us: shards(): lax.all_to_all(row_delta, 'uly', split_axis=1, concat_axis=0, tiled=True)]
    dot_general x48 -> x0, matrix products: 31.3 us -> none  [the longest x8 10.3 us: tile_stats(): jnp.einsum('qid,qcjd->qcij', query_part, key_part, preferred_element_type...]
  transfers between devices with their start and end apart: 12 -> 0, of which waited for: 7 -> 0; matrix products, arithmetic and copies ran while one was open for 15% -> 0% of each run, Pallas kernels for 0% -> 0%
where the time goes in v1:
time: 79.4 us; the launch traced here: 79 us
  Pallas kernels  71.2 us (90%)
  local copies, waits for them, and re-layouts  6.37 us (8%)
    pallas_call x1, Pallas kernels, gathered(): pl.pallas_call(functools.partial(gather_kernel, n_blk, n_uly, heads_here,...  33.8 us
    pallas_call x1, Pallas kernels, scattered(): pl.pallas_call(functools.partial(scatter_kernel, n_blk, n_uly, heads_here...  23.1 us
    pallas_call x1, Pallas kernels, grads(): pl.pallas_call(functools.partial(grads_kernel, *sizes), grid=(tiles_here,...  14.3 us
    unnamed x14, local copies, waits for them, and re-layouts  5.65 us

profile of v1, /device:TPU:0, one launch (start us, length us, event | category | flops | bytes accessed | tf_op | source)
XLA Modules:
  0.0 79.0 jit_solution(9211929535999906962)
XLA Ops:
  0.6 0.0 copy-start.3
  0.6 0.7 copy-done.3
  1.4 0.0 copy-start.4
  1.4 0.6 copy-done.4
  2.0 0.1 select_reduce_fusion
  2.1 0.0 copy-start.2
  2.2 0.6 multiply_add_fusion.code_ref
  2.8 0.1 copy-done.2
  2.8 0.1 copy.12
  3.0 0.7 reshape.19.list_ref
  3.7 33.8 %gather_heads.1 = (bf16[1024,512]{1,0:T(8,128)(2,1)}, bf16[1024,512]{1,0:T(8,128)(2,1)}, bf16[2048,128]{1,0:T(8,128)(2,1)}, bf16[2048,128]{1,0:T(8,128)(2,1)}, f32[8,4,128]{2,1,0:T(4,128)}) custom-call(bf16[128,4096]{1,0:T(8,128)(2,1)} %q_ref.1, bf16[128,4096]{1,0:T(8,128)(2,1)} %do_ref.1, bf16[128,1024]{1,0:T(8,128)(2,1)} %k_ref.1, ...), custom_call_target="tpu_custom_call" | custom-call | tf_op jit(solution)/shard_map/gather_heads/pallas_call | solution.py:151
  37.5 14.3 %tile_grads.1 = (bf16[1024,512]{1,0:T(8,128)(2,1)}, bf16[2,1024,128]{2,1,0:T(8,128)(2,1)}, f32[2,1024,128]{2,1,0:T(8,128)}) custom-call(s32[512]{0:T(512)} %reshape.19.list_ref, bf16[1024,512]{1,0:T(8,128)(2,1)} %get-tuple-element.11.q_ref, bf16[1024,512]{1,0:T(8,128)(2,1)} %get-tuple-element.12.do_ref, f32[8,4,128]{2,1,0:T(4,128)} %get-tuple-element.13.dl_ref, ...), custom_call_target="tpu_custom_call" | custom-call | flops 2684354560 | bytes 6291456 | tf_op jit(solution)/shard_map/tile_grads/pallas_call | solution.py:283
  51.8 23.1 %scatter_tokens.1 = (bf16[128,4096]{1,0:T(8,128)(2,1)}, bf16[128,1024]{1,0:T(8,128)(2,1)}, bf16[128,1024]{1,0:T(8,128)(2,1)}) custom-call(bf16[1024,512]{1,0:T(8,128)(2,1)} %get-tuple-element.16.dqh_ref, bf16[2,1024,128]{2,1,0:T(8,128)(2,1)} %get-tuple-element.17.back_ref, f32[2,1024,128]{2,1,0:T(8,128)} %get-tuple-element.18.own_ref), custom_call_target="tpu_custom_call" | custom-call | tf_op jit(solution)/shard_map/scatter_tokens/pallas_call | solution.py:444
  74.9 0.0 copy-start.1
  75.0 2.3 %copy.16 = bf16[128,4096]{1,0:T(8,128)(2,1)} copy(bf16[128,4096]{1,0:T(8,128)(2,1)} %get-tuple-element.24) | data formatting | bytes 2097152
  77.3 0.0 copy-done.1
  77.3 0.0 copy-start
  77.3 0.7 copy.17
  78.0 0.3 copy-done
  78.3 0.7 copy.18
  (2 shorter events, 0.0 us)
Async XLA Ops:
  0.6 0.7 copy-start.3
  1.4 0.7 copy-start.4
  2.1 0.7 copy-start.2
  74.9 2.3 %copy-start.1 = (bf16[128,1024]{1,0:T(8,128)(2,1)S(1)}, bf16[128,1024]{1,0:T(8,128)(2,1)}, u32[]{:S(2)}) copy-start(bf16[128,1024]{1,0:T(8,128)(2,1)} %get-tuple-element.25) | copy-start | bytes 786436
  77.3 1.0 %copy-start = (bf16[128,1024]{1,0:T(8,128)(2,1)S(1)}, bf16[128,1024]{1,0:T(8,128)(2,1)}, u32[]{:S(2)}) copy-start(bf16[128,1024]{1,0:T(8,128)(2,1)} %get-tuple-element.26) | copy-start | bytes 786436

commit v2 on v0

v2 whole, which is shorter than its diff:
```python
import functools

import jax
import jax.numpy as jnp
from jax import lax
from jax.experimental import pallas as pl
from jax.experimental.pallas import tpu as pltpu
from jax.sharding import PartitionSpec as P

DH = 128
BLOCK = 128
LANGS = 4
MASKED = -1e30
MESH = pl.DeviceIdType.MESH
LOOK = 7
VMEM_LIMIT = 56 * 1024 * 1024


def greet(b, u, n_blk, n_uly):
    barrier = pltpu.get_barrier_semaphore()
    for p in range(1, n_uly):
        pl.semaphore_signal(
            barrier, inc=1, device_id=(b, lax.rem(u + p, n_uly)), device_id_type=MESH
        )

    @pl.when(b > 0)
    def _():
        pl.semaphore_signal(barrier, inc=1, device_id=(b - 1, u), device_id_type=MESH)

    @pl.when(b < n_blk - 1)
    def _():
        pl.semaphore_signal(barrier, inc=1, device_id=(b + 1, u), device_id_type=MESH)

    ends = jnp.where(b > 0, 1, 0) + jnp.where(b < n_blk - 1, 1, 0)
    pl.semaphore_wait(barrier, n_uly - 1 + ends)


def aligned(start, size):
    return pl.ds(pl.multiple_of(start, size), size)


def partner(u, s, n):
    s = jnp.where(s == 3, 4, jnp.where(s == 4, 3, s)) if n > 4 else s
    found, bit = 0, 1
    while bit < n:
        found = found + bit * lax.rem(lax.div(u, bit) + lax.div(s, bit), 2)
        bit *= 2
    return found


def fused_kernel(
    n_blk,
    n_uly,
    tile_total,
    list_count,
    heads_here,
    repeat_count,
    list_ref,
    q_ref,
    do_ref,
    k_ref,
    v_ref,
    dl_ref,
    code_ref,
    dq_ref,
    dk_ref,
    dv_ref,
    q_all,
    do_all,
    dl_all,
    window,
    key_codes,
    acc,
    dq_all,
    back,
    returned,
    total,
    landing,
    in_send,
    in_recv,
    local_sem,
    z_send,
    z_recv,
    back_send,
    back_recv,
    out_send,
    out_recv,
    out_local,
):
    b, u = lax.axis_index("blk"), lax.axis_index("uly")
    tiles_here = n_uly
    width = heads_here * DH
    copies = repeat_count // heads_here
    direct = copies == 1
    f32 = jnp.float32
    my_cols = aligned(u * width, width)
    my_group = aligned(u * DH, DH)
    peer_of = functools.partial(partner, u, n=n_uly)

    def pieces(peer):
        group = lax.div(peer * heads_here, repeat_count)
        kv_cols = aligned(group * DH, DH)
        q_cols = aligned(peer * width, width)
        return (
            (k_ref.at[:, kv_cols], window.at[tiles_here + u, 0]),
            (v_ref.at[:, kv_cols], window.at[tiles_here + u, 1]),
            (dl_ref.at[peer], dl_all.at[u]),
            (q_ref.at[:, q_cols], q_all.at[u]),
            (do_ref.at[:, q_cols], do_all.at[u]),
        )

    def out_pieces(peer):
        if direct:
            ends = (dk_ref.at[:, my_group], dv_ref.at[:, my_group])
        else:
            ends = (landing.at[0, u], landing.at[1, u])
        return (
            (total.at[peer, 0], ends[0]),
            (total.at[peer, 1], ends[1]),
            (dq_all.at[peer], dq_ref.at[:, my_cols]),
        )

    def remote(parts, kind, s, send, recv):
        peer = peer_of(s)
        src, dst = parts(peer)[kind]
        return pltpu.make_async_remote_copy(
            src_ref=src,
            dst_ref=dst,
            send_sem=send.at[kind, s],
            recv_sem=recv.at[kind, s],
            device_id=(b, peer),
            device_id_type=MESH,
        )

    def inward(kind, s):
        return remote(pieces, kind, s, in_send, in_recv)

    def outward(kind, s):
        return remote(out_pieces, kind, s, out_send, out_recv)

    def local(kind):
        src, dst = pieces(u)[kind]
        return pltpu.make_async_copy(src, dst, local_sem.at[kind])

    def out_own(kind):
        src, dst = out_pieces(u)[kind]
        return pltpu.make_async_copy(src, dst, out_local.at[kind])

    def forward(a):
        return pltpu.make_async_remote_copy(
            src_ref=window.at[tiles_here + a],
            dst_ref=window.at[a],
            send_sem=z_send.at[a],
            recv_sem=z_recv.at[a],
            device_id=(lax.rem(b + 1, n_blk), u),
            device_id_type=MESH,
        )

    def backward(a):
        return pltpu.make_async_remote_copy(
            src_ref=back.at[a],
            dst_ref=returned.at[a],
            send_sem=back_send.at[a],
            recv_sem=back_recv.at[a],
            device_id=(lax.rem(b + n_blk - 1, n_blk), u),
            device_id_type=MESH,
        )

    def each(first, last, body):
        lax.fori_loop(first, last, lambda s, _: (body(s), 0)[1], 0)

    has_next = b < n_blk - 1
    has_prev = b > 0

    for kind in range(5):
        local(kind).start()
    greet(b, u, n_blk, n_uly)

    def send_keys(s):
        inward(0, s).start()
        inward(1, s).start()

    def send_rows(s):
        inward(2, s).start()
        inward(3, s).start()
        inward(4, s).start()

    each(1, n_uly, send_keys)
    each(1, min(LOOK, n_uly - 1) + 1, send_rows)
    local(0).wait()
    local(1).wait()

    @pl.when(has_next)
    def _():
        forward(u).start()

    def prepare(t):
        key_codes[t] = jnp.broadcast_to(code_ref[pl.ds(t, 1), :], (BLOCK, BLOCK)).T
        acc[t] = jnp.zeros(acc.shape[1:], f32)

    each(0, 2 * tiles_here, prepare)

    @pl.when(b == 0)
    def _():
        window[0:tiles_here] = jnp.zeros((tiles_here,) + window.shape[1:], window.dtype)

    def pass_on(s):
        inward(0, s).wait_recv()
        inward(1, s).wait_recv()

        @pl.when(has_next)
        def _():
            forward(peer_of(s)).start()

    each(1, n_uly, pass_on)

    @pl.when(has_prev)
    def _():
        each(0, tiles_here, lambda a: forward(a).wait_recv())

    local(2).wait()
    local(3).wait()
    local(4).wait()

    scaling = float(DH) ** (-0.5)
    across = (((1,), (1,)), ((), ()))
    gap = lax.broadcasted_iota(jnp.int32, (BLOCK, BLOCK), 0) - lax.broadcasted_iota(
        jnp.int32, (BLOCK, BLOCK), 1
    )
    group_here = lax.div(u * heads_here, repeat_count)

    def tile_work(a):
        tile = b * tiles_here + a
        base = (group_here * tile_total + tile) * list_count
        listed = [list_ref[base + l] for l in range(list_count)]
        cands = [tile - 1, tile] + listed
        own_slot = tiles_here + a
        window_first = (b - 1) * tiles_here
        query_code = code_ref[pl.ds(own_slot, 1), :]
        query_lang = query_code & (LANGS - 1)
        slots = []
        biases = []
        for c, cand in enumerate(cands):
            usable = cand >= 0
            for other in cands[: c if c >= 2 else 0]:
                usable = usable & (cand != other)
            marked = cand == listed[0]
            for other in listed[1:]:
                marked = marked | (cand == other)
            if c < 2:
                slot = own_slot - 1 + c
            else:
                slot = jnp.clip(cand - window_first, 0, 2 * tiles_here - 1)
            limit = jnp.where(usable, (tile - cand) * BLOCK, -2 * BLOCK)
            seen_lang = jnp.where(marked, query_lang, -1)
            key_code = key_codes[slot]
            allowed = (gap <= limit) & (
                (key_code == query_code) | ((key_code & (LANGS - 1)) == seen_lang)
            )
            slots.append(slot)
            biases.append(jnp.where(allowed, 0.0, MASKED))

        def stacked(rows):
            return jnp.concatenate([rows[:, h * DH : (h + 1) * DH] for h in range(heads_here)], 0)

        bias = jnp.concatenate(biases, axis=0)
        bias = jnp.concatenate([bias] * heads_here, axis=1)
        key_part = jnp.concatenate([window[s, 0] for s in slots], axis=0)
        value_part = jnp.concatenate([window[s, 1] for s in slots], axis=0)
        query_part = stacked(q_all[a])
        dout_part = stacked(do_all[a])
        delta_tile = dl_all[a]
        delta = jnp.concatenate([delta_tile[h : h + 1, :] for h in range(heads_here)], axis=1)
        scores = lax.dot_general(key_part, query_part, across, preferred_element_type=f32)
        scores = scores * scaling + bias
        top = jnp.max(scores, axis=0, keepdims=True)
        raised = jnp.exp(scores - top)
        weights = raised * (1.0 / jnp.sum(raised, axis=0, keepdims=True))
        grad_weights = lax.dot_general(value_part, dout_part, across, preferred_element_type=f32)
        grad_scores = (weights * (grad_weights - delta)).astype(jnp.bfloat16)
        grad_query = scaling * lax.dot_general(
            grad_scores, key_part, (((0,), (0,)), ((), ())), preferred_element_type=f32
        )
        for h in range(heads_here):
            dq_all[a, :, h * DH : (h + 1) * DH] = grad_query[h * BLOCK : (h + 1) * BLOCK].astype(
                dq_all.dtype
            )
        grad_key = scaling * jnp.dot(grad_scores, query_part, preferred_element_type=f32)
        grad_value = jnp.dot(weights.astype(jnp.bfloat16), dout_part, preferred_element_type=f32)
        parts = (grad_key, grad_value)
        for c in range(2):
            for k in range(2):
                acc[slots[c], k] += parts[k][c * BLOCK : (c + 1) * BLOCK]

        def spread(t):
            for k in range(2):
                more = acc[t, k]
                for c in range(2, 2 + list_count):
                    piece = parts[k][c * BLOCK : (c + 1) * BLOCK]
                    more = more + jnp.where(slots[c] == t, piece, 0.0)
                acc[t, k] = more

        each(0, 2 * tiles_here, spread)

    tile_work(u)
    out_own(2).start()

    def step(s):
        @pl.when(s + LOOK < n_uly)
        def _():
            send_rows(s + LOOK)

        inward(2, s).wait_recv()
        inward(3, s).wait_recv()
        inward(4, s).wait_recv()
        tile_work(peer_of(s))
        outward(2, s).start()

    each(1, n_uly, step)

    @pl.when(has_prev)
    def _():
        def give_back(s):
            a = peer_of(s)
            back[a] = acc[a].astype(back.dtype)
            backward(a).start()

        each(0, n_uly, give_back)

    def settle(s):
        a = peer_of(s)

        @pl.when(has_next)
        def _():
            backward(a).wait_recv()
            total[a] = (acc[tiles_here + a] + returned[a].astype(f32)).astype(total.dtype)

        @pl.when(b == n_blk - 1)
        def _():
            total[a] = acc[tiles_here + a].astype(total.dtype)

    settle(0)
    out_own(0).start()
    out_own(1).start()

    def settle_and_send(s):
        settle(s)
        outward(0, s).start()
        outward(1, s).start()

    each(1, n_uly, settle_and_send)

    for kind in range(3):
        out_own(kind).wait()

    def finish(s):
        for kind in range(3):
            outward(kind, s).wait_recv()
        for kind in range(5):
            inward(kind, s).wait_send()
        for kind in range(3):
            outward(kind, s).wait_send()

    each(1, n_uly, finish)

    @pl.when(has_next)
    def _():
        each(0, n_uly, lambda a: forward(a).wait_send())

    @pl.when(has_prev)
    def _():
        each(0, n_uly, lambda a: backward(a).wait_send())

    if not direct:
        for kind, out in ((0, dk_ref), (1, dv_ref)):
            for g in range(n_uly // copies):
                summed = landing[kind, g * copies].astype(f32)
                for r in range(1, copies):
                    summed = summed + landing[kind, g * copies + r].astype(f32)
                out[:, g * DH : (g + 1) * DH] = summed.astype(out.dtype)


def window_codes(doc_ids, doc_lang, row_count):
    block_index = lax.axis_index("blk")
    earlier = lax.dynamic_slice_in_dim(
        doc_ids, jnp.maximum(block_index - 1, 0) * row_count, row_count
    )
    here = lax.dynamic_slice_in_dim(doc_ids, block_index * row_count, row_count)
    docs = jnp.concatenate([earlier, here]).reshape(-1, BLOCK)
    numbers = jnp.arange(doc_lang.shape[0], dtype=jnp.int32)
    hit = docs[None] == numbers[:, None, None]
    lang = jnp.sum(jnp.where(hit, doc_lang[:, None, None], 0), axis=0)
    return docs * LANGS + lang


def shards(queries, keys, values, grad_out, row_delta, doc_ids, doc_lang, tile_list):
    tok_count, full_width = queries.shape
    heads_all = full_width // DH
    groups_all = keys.shape[1] // DH
    repeat_count = heads_all // groups_all
    n_uly = lax.axis_size("uly")
    n_blk = lax.axis_size("blk")
    heads_here = heads_all // n_uly
    width = heads_here * DH
    copies = repeat_count // heads_here
    row_count = tok_count * n_uly
    delta_rows = row_delta.T.reshape(n_uly, heads_here, tok_count)
    codes = window_codes(doc_ids, doc_lang, row_count)
    anywhere = pl.BlockSpec(memory_space=pl.ANY)
    in_vmem = pl.BlockSpec(memory_space=pltpu.VMEM)
    kv_spec = in_vmem if copies > 1 else anywhere
    bf16, f32 = jnp.bfloat16, jnp.float32
    pair = (2, BLOCK, DH)
    dma = pltpu.SemaphoreType.DMA
    return pl.pallas_call(
        functools.partial(
            fused_kernel,
            n_blk,
            n_uly,
            tile_list.shape[1],
            tile_list.shape[2],
            heads_here,
            repeat_count,
        ),
        out_shape=(
            jax.ShapeDtypeStruct(queries.shape, bf16),
            jax.ShapeDtypeStruct(keys.shape, bf16),
            jax.ShapeDtypeStruct(values.shape, bf16),
        ),
        in_specs=[pl.BlockSpec(memory_space=pltpu.SMEM)] + [anywhere] * 5 + [in_vmem],
        out_specs=(anywhere, kv_spec, kv_spec),
        scratch_shapes=[
            pltpu.VMEM((n_uly, BLOCK, width), bf16),
            pltpu.VMEM((n_uly, BLOCK, width), bf16),
            pltpu.VMEM((n_uly, heads_here, BLOCK), f32),
            pltpu.VMEM((2 * n_uly,) + pair, bf16),
            pltpu.VMEM((2 * n_uly, BLOCK, BLOCK), jnp.int32),
            pltpu.VMEM((2 * n_uly,) + pair, f32),
            pltpu.VMEM((n_uly, BLOCK, width), bf16),
            pltpu.VMEM((n_uly,) + pair, bf16),
            pltpu.VMEM((n_uly,) + pair, bf16),
            pltpu.VMEM((n_uly,) + pair, bf16),
            pltpu.VMEM((2, n_uly if copies > 1 else 1, BLOCK, DH), bf16),
            dma((5, n_uly)),
            dma((5, n_uly)),
            dma((5,)),
            dma((n_uly,)),
            dma((n_uly,)),
            dma((n_uly,)),
            dma((n_uly,)),
            dma((3, n_uly)),
            dma((3, n_uly)),
            dma((3,)),
        ],
        compiler_params=pltpu.CompilerParams(
            collective_id=0, has_side_effects=True, vmem_limit_bytes=VMEM_LIMIT
        ),
        name="attention_grads",
    )(tile_list.reshape(-1), queries, grad_out, keys, values, delta_rows, codes)


def solution(mesh):
    placed = (
        P(("blk", "uly"), None),
        P(("blk", "uly"), None),
        P(("blk", "uly"), None),
        P(("blk", "uly"), None),
        P(("blk", "uly"), None),
        P(),
        P(),
        P(),
    )
    return jax.shard_map(
        shards,
        mesh=mesh,
        in_specs=placed,
        out_specs=(P(("blk", "uly"), None), P(("blk", "uly"), None), P(("blk", "uly"), None)),
        check_vma=False,
    )
```

time: 961 us -> 64.9 us (0.07)
  local copies, waits for them, and re-layouts: 590 us -> 6.37 us
  other arithmetic: 138 us -> 0.74 us
  waiting for transfers between devices: 128 us -> 0 us
  Pallas kernels: 0 us -> 56.7 us
  starting transfers between devices: 43 us -> 0 us
  matrix products: 31.3 us -> 0 us
  loops' own time: 23.7 us -> 0 us
    gather x124 -> x0, local copies, waits for them, and re-layouts: 515 us -> none  [the longest x16 189 us: allowed_tiles(): key_doc = jnp.take(doc_ids, key_pos, mode='clip')]
    ppermute x4 -> x0, waiting for transfers between devices: 77 us -> none  [from_behind(): return lax.ppermute(block, axis, route)]
    pallas_call x0 -> x1, Pallas kernels: none -> 56.7 us  [shards(): pl.pallas_call(functools.partial(fused_kernel, n_blk, n_uly, tile_list.sh...]
    scatter-add x16 -> x0, other arithmetic: 54.5 us -> none  [the longest x8 27.3 us: scan_step(): key_sum = key_sum.at[flat_slot].add(grad_key.reshape(-1, BLOCK, DH))]
    all_to_all x8 -> x0, waiting for transfers between devices: 50.6 us -> none  [the longest x1 14.2 us: shards(): lax.all_to_all(widened(keys, groups_all, repeat_count), 'uly', split_axis...]
    gather x65 -> x0, other arithmetic: 40.4 us -> none  [the longest x1 39.9 us: shards(): position_lang = jnp.take(doc_lang, doc_ids, mode='clip')]
    all_to_all x8 -> x0, starting transfers between devices: 31.8 us -> none  [the longest x1 5.31 us: shards(): lax.all_to_all(row_delta, 'uly', split_axis=1, concat_axis=0, tiled=True)]
    dot_general x48 -> x0, matrix products: 31.3 us -> none  [the longest x8 10.3 us: tile_stats(): jnp.einsum('qid,qcjd->qcij', query_part, key_part, preferred_element_type...]
  transfers between devices with their start and end apart: 12 -> 0, of which waited for: 7 -> 0; matrix products, arithmetic and copies ran while one was open for 15% -> 0% of each run, Pallas kernels for 0% -> 0%
where the time goes in v2:
time: 64.9 us; the launch traced here: 64.5 us
  Pallas kernels  56.7 us (87%)
  local copies, waits for them, and re-layouts  6.37 us (10%)
  other arithmetic  0.74 us (1%)
  between operations  0.68 us (1%)
    pallas_call x1, Pallas kernels, shards(): pl.pallas_call(functools.partial(fused_kernel, n_blk, n_uly, tile_list.sh...  56.7 us
    unnamed x14, local copies, waits for them, and re-layouts  5.65 us

profile of v2, /device:TPU:0, one launch (start us, length us, event | category | flops | bytes accessed | tf_op | source)
XLA Modules:
  0.0 64.5 jit_solution(17207736050987767207)
XLA Ops:
  0.6 0.0 copy-start.3
  0.6 0.7 %copy-done.3 = s32[4096]{0:T(1024)S(1)} copy-done((s32[4096]{0:T(1024)S(1)}, s32[4096]{0:T(1024)}, u32[]{:S(2)}) %copy-start.3) | copy-done | bytes 16408
  1.4 0.0 copy-start.4
  1.4 0.6 %copy-done.4 = s32[64]{0:T(128)S(1)} copy-done((s32[64]{0:T(128)S(1)}, s32[64]{0:T(128)}, u32[]{:S(2)}) %copy-start.4) | copy-done | bytes 280
  2.0 0.1 select_reduce_fusion
  2.1 0.0 copy-start.2
  2.2 0.6 multiply_add_fusion.code_ref
  2.8 0.1 copy-done.2
  2.8 0.1 copy.12
  3.0 0.7 %reshape.19.list_ref = s32[512]{0:T(512)} reshape(s32[8,32,2]{2,1,0:T(8,128)S(1)} %copy.12) | data formatting | bytes 4096 | tf_op jit(solution)/shard_map/reshape | solution.py:459
  3.7 56.7 %attention_grads.1 = (bf16[128,4096]{1,0:T(8,128)(2,1)}, bf16[128,1024]{1,0:T(8,128)(2,1)}, bf16[128,1024]{1,0:T(8,128)(2,1)}) custom-call(s32[512]{0:T(512)} %reshape.19.list_ref, bf16[128,4096]{1,0:T(8,128)(2,1)} %q_ref.1, bf16[128,4096]{1,0:T(8,128)(2,1)} %do_ref.1, bf16[128,1024]{1,0:T(8,128)(2,1)} %k_ref.1, bf16[128,1024]{1,0:T(8,128)(2,1)} %v_ref.1, ...), custom_call_target="tpu_custom_call" | custom-call | tf_op jit(solution)/shard_map/attention_grads/pallas_call | solution.py:415
  60.4 0.0 copy-start.1
  60.4 2.3 %copy.16 = bf16[128,4096]{1,0:T(8,128)(2,1)} copy(bf16[128,4096]{1,0:T(8,128)(2,1)} %get-tuple-element.8) | data formatting | bytes 2097152
  62.7 0.0 copy-done.1
  62.7 0.0 copy-start
  62.7 0.7 %copy.17 = bf16[128,1024]{1,0:T(8,128)(2,1)} copy(bf16[128,1024]{1,0:T(8,128)(2,1)S(1)} %copy-done.1) | data formatting | bytes 524288
  63.5 0.3 copy-done
  63.8 0.7 %copy.18 = bf16[128,1024]{1,0:T(8,128)(2,1)} copy(bf16[128,1024]{1,0:T(8,128)(2,1)S(1)} %copy-done) | data formatting | bytes 524288
  (2 shorter events, 0.0 us)
Async XLA Ops:
  0.6 0.7 %copy-start.3 = (s32[4096]{0:T(1024)S(1)}, s32[4096]{0:T(1024)}, u32[]{:S(2)}) copy-start(s32[4096]{0:T(1024)} %param.13) | copy-start | bytes 49156
  1.4 0.7 %copy-start.4 = (s32[64]{0:T(128)S(1)}, s32[64]{0:T(128)}, u32[]{:S(2)}) copy-start(s32[64]{0:T(128)} %param.14) | copy-start | bytes 772
  2.1 0.7 %copy-start.2 = (s32[8,32,2]{1,2,0:T(2,128)S(1)}, s32[8,32,2]{1,2,0:T(2,128)}, u32[]{:S(2)}) copy-start(s32[8,32,2]{1,2,0:T(2,128)} %param.15) | copy-start | bytes 6148
  60.4 2.3 %copy-start.1 = (bf16[128,1024]{1,0:T(8,128)(2,1)S(1)}, bf16[128,1024]{1,0:T(8,128)(2,1)}, u32[]{:S(2)}) copy-start(bf16[128,1024]{1,0:T(8,128)(2,1)} %get-tuple-element.9) | copy-start | bytes 786436
  62.7 1.0 %copy-start = (bf16[128,1024]{1,0:T(8,128)(2,1)S(1)}, bf16[128,1024]{1,0:T(8,128)(2,1)}, u32[]{:S(2)}) copy-start(bf16[128,1024]{1,0:T(8,128)(2,1)} %get-tuple-element.10) | copy-start | bytes 786436

commit v3 on v2

--- a/solution.py
+++ b/solution.py
@@ -51,17 +51,17 @@
 def fused_kernel(
     n_blk,
     n_uly,
-    tile_total,
     list_count,
     heads_here,
     repeat_count,
-    list_ref,
+    list_hbm,
+    lang_hbm,
+    docs_hbm,
     q_ref,
     do_ref,
     k_ref,
     v_ref,
     dl_ref,
-    code_ref,
     dq_ref,
     dk_ref,
     dv_ref,
@@ -69,6 +69,9 @@
     do_all,
     dl_all,
     window,
+    list_ref,
+    lang_ref,
+    code_ref,
     key_codes,
     acc,
     dq_all,
@@ -86,6 +89,7 @@
     out_send,
     out_recv,
     out_local,
+    table_sem,
 ):
     b, u = lax.axis_index("blk"), lax.axis_index("uly")
     tiles_here = n_uly
@@ -172,8 +176,24 @@
     has_next = b < n_blk - 1
     has_prev = b > 0
 
+    tables = (
+        pltpu.make_async_copy(list_hbm, list_ref, table_sem.at[0]),
+        pltpu.make_async_copy(lang_hbm, lang_ref, table_sem.at[1]),
+        pltpu.make_async_copy(
+            docs_hbm.at[aligned(jnp.maximum(b - 1, 0) * tiles_here, tiles_here), :],
+            code_ref.at[pl.ds(0, tiles_here), :],
+            table_sem.at[2],
+        ),
+        pltpu.make_async_copy(
+            docs_hbm.at[aligned(b * tiles_here, tiles_here), :],
+            code_ref.at[pl.ds(tiles_here, tiles_here), :],
+            table_sem.at[3],
+        ),
+    )
     for kind in range(5):
         local(kind).start()
+    for table in tables:
+        table.start()
     greet(b, u, n_blk, n_uly)
 
     def send_keys(s):
@@ -193,6 +213,16 @@
     @pl.when(has_next)
     def _():
         forward(u).start()
+
+    for table in tables:
+        table.wait()
+    docs = code_ref[...]
+
+    def look_up(d, lang):
+        return lang + jnp.where(docs == d, lang_ref[d], 0)
+
+    lang = lax.fori_loop(0, lang_ref.shape[0], look_up, jnp.zeros_like(docs))
+    code_ref[...] = docs * LANGS + lang
 
     def prepare(t):
         key_codes[t] = jnp.broadcast_to(code_ref[pl.ds(t, 1), :], (BLOCK, BLOCK)).T
@@ -231,8 +261,7 @@
 
     def tile_work(a):
         tile = b * tiles_here + a
-        base = (group_here * tile_total + tile) * list_count
-        listed = [list_ref[base + l] for l in range(list_count)]
+        listed = [list_ref[group_here, l, tile] for l in range(list_count)]
         cands = [tile - 1, tile] + listed
         own_slot = tiles_here + a
         window_first = (b - 1) * tiles_here
@@ -380,17 +409,52 @@
                 out[:, g * DH : (g + 1) * DH] = summed.astype(out.dtype)
 
 
-def window_codes(doc_ids, doc_lang, row_count):
-    block_index = lax.axis_index("blk")
-    earlier = lax.dynamic_slice_in_dim(
-        doc_ids, jnp.maximum(block_index - 1, 0) * row_count, row_count
-    )
-    here = lax.dynamic_slice_in_dim(doc_ids, block_index * row_count, row_count)
-    docs = jnp.concatenate([earlier, here]).reshape(-1, BLOCK)
-    numbers = jnp.arange(doc_lang.shape[0], dtype=jnp.int32)
-    hit = docs[None] == numbers[:, None, None]
-    lang = jnp.sum(jnp.where(hit, doc_lang[:, None, None], 0), axis=0)
-    return docs * LANGS + lang
+def hand_over_kernel(*refs):
+    count = len(refs) // 2
+    sems = refs[-1]
+    moves = []
+    for k in range(count):
+        src, dst = refs[k], refs[count + k]
+        half = src.shape[0] // 2
+        for part in range(2):
+            rows = pl.ds(part * half, half)
+            moves.append(
+                pltpu.make_async_copy(src.at[rows, :], dst.at[rows, :], sems.at[2 * k + part])
+            )
+    for move in moves:
+        move.start()
+    for move in moves:
+        move.wait()
+
+
+def handed_over(arrays):
+    anywhere = pl.BlockSpec(memory_space=pl.ANY)
+    return pl.pallas_call(
+        hand_over_kernel,
+        out_shape=tuple(jax.ShapeDtypeStruct(x.shape, x.dtype) for x in arrays),
+        in_specs=[anywhere] * len(arrays),
+        out_specs=(anywhere,) * len(arrays),
+        scratch_shapes=[pltpu.SemaphoreType.DMA((2 * len(arrays),))],
+        name="hand_over",
+    )(*arrays)
+
+
+def copy_body(*refs):
+    count = len(refs) // 2
+    for k in range(count):
+        refs[count + k][...] = refs[k][...]
+
+
+def handed_over_v(arrays):
+    specs = [pl.BlockSpec((64, x.shape[1]), lambda i: (i, 0)) for x in arrays]
+    return pl.pallas_call(
+        copy_body,
+        grid=(arrays[0].shape[0] // 64,),
+        out_shape=tuple(jax.ShapeDtypeStruct(x.shape, x.dtype) for x in arrays),
+        in_specs=specs,
+        out_specs=tuple(specs),
+        name="hand_over",
+    )(*arrays)
 
 
 def shards(queries, keys, values, grad_out, row_delta, doc_ids, doc_lang, tile_list):
@@ -403,21 +467,20 @@
     heads_here = heads_all // n_uly
     width = heads_here * DH
     copies = repeat_count // heads_here
-    row_count = tok_count * n_uly
+    lists = tile_list.transpose(0, 2, 1)
+    docs = doc_ids.reshape(-1, BLOCK)
     delta_rows = row_delta.T.reshape(n_uly, heads_here, tok_count)
-    codes = window_codes(doc_ids, doc_lang, row_count)
     anywhere = pl.BlockSpec(memory_space=pl.ANY)
     in_vmem = pl.BlockSpec(memory_space=pltpu.VMEM)
     kv_spec = in_vmem if copies > 1 else anywhere
     bf16, f32 = jnp.bfloat16, jnp.float32
     pair = (2, BLOCK, DH)
     dma = pltpu.SemaphoreType.DMA
-    return pl.pallas_call(
+    outs = pl.pallas_call(
         functools.partial(
             fused_kernel,
             n_blk,
             n_uly,
-            tile_list.shape[1],
             tile_list.shape[2],
             heads_here,
             repeat_count,
@@ -427,13 +490,16 @@
             jax.ShapeDtypeStruct(keys.shape, bf16),
             jax.ShapeDtypeStruct(values.shape, bf16),
         ),
-        in_specs=[pl.BlockSpec(memory_space=pltpu.SMEM)] + [anywhere] * 5 + [in_vmem],
+        in_specs=[anywhere] * 8,
         out_specs=(anywhere, kv_spec, kv_spec),
         scratch_shapes=[
             pltpu.VMEM((n_uly, BLOCK, width), bf16),
             pltpu.VMEM((n_uly, BLOCK, width), bf16),
             pltpu.VMEM((n_uly, heads_here, BLOCK), f32),
             pltpu.VMEM((2 * n_uly,) + pair, bf16),
+            pltpu.SMEM(lists.shape, jnp.int32),
+            pltpu.SMEM(doc_lang.shape, jnp.int32),
+            pltpu.VMEM((2 * n_uly, BLOCK), jnp.int32),
             pltpu.VMEM((2 * n_uly, BLOCK, BLOCK), jnp.int32),
             pltpu.VMEM((2 * n_uly,) + pair, f32),
             pltpu.VMEM((n_uly, BLOCK, width), bf16),
@@ -451,12 +517,14 @@
             dma((3, n_uly)),
             dma((3, n_uly)),
             dma((3,)),
+            dma((4,)),
         ],
         compiler_params=pltpu.CompilerParams(
             collective_id=0, has_side_effects=True, vmem_limit_bytes=VMEM_LIMIT
         ),
         name="attention_grads",
-    )(tile_list.reshape(-1), queries, grad_out, keys, values, delta_rows, codes)
+    )(lists, doc_lang, docs, queries, grad_out, keys, values, delta_rows)
+    return handed_over_v(outs)
 
 
 def solution(mesh):

time: 64.9 us -> 59.2 us (0.912)
  local copies, waits for them, and re-layouts: 6.37 us -> 0 us
  Pallas kernels: 56.7 us -> 58.4 us
  other arithmetic: 0.74 us -> 0 us
    unnamed x14 -> x0, local copies, waits for them, and re-layouts: 5.65 us -> none
    pallas_call x0 -> x1, Pallas kernels: none -> 2.33 us  [handed_over_v(): pl.pallas_call(copy_body, grid=(arrays[0].shape[0] // 64,), out_shape=tup...]
    reshape x1 -> x0, local copies, waits for them, and re-layouts: 0.72 us -> none  [shards(): tile_list.reshape(-1)]
where the time goes in v3:
time: 59.2 us; the launch traced here: 59.1 us
  Pallas kernels  58.4 us (99%)
  between operations  0.64 us (1%)
    pallas_call x1, Pallas kernels, shards(): pl.pallas_call(functools.partial(fused_kernel, n_blk, n_uly, tile_list.sh...  56.1 us
    pallas_call x1, Pallas kernels, handed_over_v(): pl.pallas_call(copy_body, grid=(arrays[0].shape[0] // 64,), out_shape=tup...  2.33 us

profile of v3, /device:TPU:0, one launch (start us, length us, event | category | flops | bytes accessed | tf_op | source)
XLA Modules:
  0.0 59.1 jit_solution(12006016197697067879)
XLA Ops:
  0.6 56.1 %attention_grads.1 = (bf16[128,4096]{1,0:T(8,128)(2,1)}, bf16[128,1024]{1,0:T(8,128)(2,1)}, bf16[128,1024]{1,0:T(8,128)(2,1)}) custom-call(s32[8,2,32]{2,1,0:T(2,128)} %bitcast.7, s32[64]{0:T(128)} %lang_hbm.1, s32[32,128]{1,0:T(8,128)} %bitcast.5, bf16[128,4096]{1,0:T(8,128)(2,1)} %q_ref.1, bf16[128,4096]{1,0:T(8,128)(2,1)} %do_ref.1, ...), custom_call_target="tpu_custom_call" | custom-call | tf_op jit(solution)/shard_map/attention_grads/pallas_call | solution.py:479
  56.7 2.3 %hand_over.1 = (bf16[128,4096]{1,0:T(8,128)(2,1)}, bf16[128,1024]{1,0:T(8,128)(2,1)}, bf16[128,1024]{1,0:T(8,128)(2,1)}) custom-call(bf16[128,4096]{1,0:T(8,128)(2,1)} %get-tuple-element.6.refs_0_, bf16[128,1024]{1,0:T(8,128)(2,1)} %get-tuple-element.7.refs_1_, bf16[128,1024]{1,0:T(8,128)(2,1)} %get-tuple-element.8.refs_2_), custom_call_target="tpu_custom_call" | custom-call | tf_op jit(solution)/shard_map/hand_over/pallas_call | solution.py:450

commit v4 on v3

--- a/solution.py
+++ b/solution.py
@@ -13,6 +13,7 @@
 MASKED = -1e30
 MESH = pl.DeviceIdType.MESH
 LOOK = 7
+CHUNKS = 4
 VMEM_LIMIT = 56 * 1024 * 1024
 
 
@@ -40,7 +41,6 @@
 
 
 def partner(u, s, n):
-    s = jnp.where(s == 3, 4, jnp.where(s == 4, 3, s)) if n > 4 else s
     found, bit = 0, 1
     while bit < n:
         found = found + bit * lax.rem(lax.div(u, bit) + lax.div(s, bit), 2)
@@ -410,49 +410,39 @@
 
 
 def hand_over_kernel(*refs):
-    count = len(refs) // 2
-    sems = refs[-1]
+    count = (len(refs) - 2) // 3
+    in_sem, out_sem = refs[-2:]
     moves = []
     for k in range(count):
-        src, dst = refs[k], refs[count + k]
-        half = src.shape[0] // 2
-        for part in range(2):
-            rows = pl.ds(part * half, half)
+        src, dst, held = refs[k], refs[count + k], refs[2 * count + k]
+        part = src.shape[0] // CHUNKS
+        for c in range(CHUNKS):
+            rows = pl.ds(c * part, part)
             moves.append(
-                pltpu.make_async_copy(src.at[rows, :], dst.at[rows, :], sems.at[2 * k + part])
+                (
+                    pltpu.make_async_copy(src.at[rows, :], held.at[rows, :], in_sem.at[k, c]),
+                    pltpu.make_async_copy(held.at[rows, :], dst.at[rows, :], out_sem.at[k, c]),
+                )
             )
-    for move in moves:
-        move.start()
-    for move in moves:
-        move.wait()
+    for fetch, _ in moves:
+        fetch.start()
+    for fetch, store in moves:
+        fetch.wait()
+        store.start()
+    for _, store in moves:
+        store.wait()
 
 
 def handed_over(arrays):
     anywhere = pl.BlockSpec(memory_space=pl.ANY)
+    count = len(arrays)
     return pl.pallas_call(
         hand_over_kernel,
         out_shape=tuple(jax.ShapeDtypeStruct(x.shape, x.dtype) for x in arrays),
-        in_specs=[anywhere] * len(arrays),
-        out_specs=(anywhere,) * len(arrays),
-        scratch_shapes=[pltpu.SemaphoreType.DMA((2 * len(arrays),))],
-        name="hand_over",
-    )(*arrays)
-
-
-def copy_body(*refs):
-    count = len(refs) // 2
-    for k in range(count):
-        refs[count + k][...] = refs[k][...]
-
-
-def handed_over_v(arrays):
-    specs = [pl.BlockSpec((64, x.shape[1]), lambda i: (i, 0)) for x in arrays]
-    return pl.pallas_call(
-        copy_body,
-        grid=(arrays[0].shape[0] // 64,),
-        out_shape=tuple(jax.ShapeDtypeStruct(x.shape, x.dtype) for x in arrays),
-        in_specs=specs,
-        out_specs=tuple(specs),
+        in_specs=[anywhere] * count,
+        out_specs=(anywhere,) * count,
+        scratch_shapes=[pltpu.VMEM(x.shape, x.dtype) for x in arrays]
+        + [pltpu.SemaphoreType.DMA((count, CHUNKS)), pltpu.SemaphoreType.DMA((count, CHUNKS))],
         name="hand_over",
     )(*arrays)
 
@@ -524,7 +514,7 @@
         ),
         name="attention_grads",
     )(lists, doc_lang, docs, queries, grad_out, keys, values, delta_rows)
-    return handed_over_v(outs)
+    return handed_over(outs)
 
 
 def solution(mesh):

time: 59.2 us -> 59.2 us (level)
  no operation moved by 1% of the time
where the time goes in v4:
time: 59.2 us; the launch traced here: 59 us
  Pallas kernels  58.4 us (99%)
  between operations  0.64 us (1%)
    pallas_call x1, Pallas kernels, shards(): pl.pallas_call(functools.partial(fused_kernel, n_blk, n_uly, tile_list.sh...  56.1 us
    pallas_call x1, Pallas kernels, handed_over(): pl.pallas_call(hand_over_kernel, out_shape=tuple((jax.ShapeDtypeStruct(x....  2.28 us

profile of v4, /device:TPU:0, one launch (start us, length us, event | category | flops | bytes accessed | tf_op | source)
XLA Modules:
  0.0 59.0 jit_solution(2616520881957271235)
XLA Ops:
  0.6 56.1 %attention_grads.1 = (bf16[128,4096]{1,0:T(8,128)(2,1)}, bf16[128,1024]{1,0:T(8,128)(2,1)}, bf16[128,1024]{1,0:T(8,128)(2,1)}) custom-call(s32[8,2,32]{2,1,0:T(2,128)} %bitcast.7, s32[64]{0:T(128)} %lang_hbm.1, s32[32,128]{1,0:T(8,128)} %bitcast.5, bf16[128,4096]{1,0:T(8,128)(2,1)} %q_ref.1, bf16[128,4096]{1,0:T(8,128)(2,1)} %do_ref.1, ...), custom_call_target="tpu_custom_call" | custom-call | tf_op jit(solution)/shard_map/attention_grads/pallas_call | solution.py:469
  56.7 2.3 %hand_over.1 = (bf16[128,4096]{1,0:T(8,128)(2,1)}, bf16[128,1024]{1,0:T(8,128)(2,1)}, bf16[128,1024]{1,0:T(8,128)(2,1)}) custom-call(bf16[128,4096]{1,0:T(8,128)(2,1)} %get-tuple-element.6.refs_0_, bf16[128,1024]{1,0:T(8,128)(2,1)} %get-tuple-element.7.refs_1_, bf16[128,1024]{1,0:T(8,128)(2,1)} %get-tuple-element.8.refs_2_), custom_call_target="tpu_custom_call" | custom-call | tf_op jit(solution)/shard_map/hand_over/pallas_call | solution.py:439
